TPU v7x, 32 devices: a whole 2x2x4 slice. The times are simulated.
32 devices in a mesh: section: 4 (over z), expert: 4 (over y, x), dp: 2 (over core).
Axes of the slice: x: 2, y: 2, z: 4, core: 2. Of those that a mesh axis runs over, the one named last changes fastest.
Arguments:
- tokens: bfloat16 [2, 512, 2048], P(None, ('expert', 'dp')), may hold values from -24 to 24
- expert_ids: int32 [4, 2, 512, 4], P('section', None, ('expert', 'dp')), may hold values from 0 to 7, all different within a row; in each aligned block of 64 rows (0 to 63, 64 to 127, ..., all dimensions but the last counted through in order) at most 64 rows name the same one
- labels: int32 [2, 512], P(None, ('expert', 'dp')), may hold values from 0 to 127
- router: bfloat16 [4, 2048, 8], P('section'), may hold values from -0.125 to 0.125
- class_head: bfloat16 [2048, 128], replicated, may hold values from -0.5 to 0.5
- w_gate: bfloat16 [4, 8, 2048, 768], P('section', ('expert', 'dp')), may hold values from -0.125 to 0.125
- w_up: bfloat16 [4, 8, 2048, 768], P('section', ('expert', 'dp')), may hold values from -0.125 to 0.125
- w_down: bfloat16 [4, 8, 768, 2048], P('section', ('expert', 'dp')), may hold values from -0.21875 to 0.21875
Outputs:
- mean_loss: float32 [], replicated
- grad_head: float32 [2048, 128], replicated
- grad_router: float32 [4, 2048, 8], P('section')
- grad_gate: bfloat16 [4, 8, 2048, 768], P('section', ('expert', 'dp'))
- grad_up: bfloat16 [4, 8, 2048, 768], P('section', ('expert', 'dp'))
- grad_down: bfloat16 [4, 8, 768, 2048], P('section', ('expert', 'dp'))
Inputs may be any that keep to these rules, and one draw needn't show every extreme that they name: `expert_ids`: each token names 4 different experts; among the 64 tokens of one device in one micro-batch and layer no expert is named more than 64 times, a bound that some block reaches.
All inputs are finite; a program needn't handle non-finite values.
Results may differ from a plain program's by a relative error of at most 0.025.
Values may be sent and summed in bfloat16 or wider, within the bound.
A program may use at most 320 MiB of HBM per device.

v0:
```python
import jax
import jax.numpy as jnp
from jax import lax
from jax.sharding import PartitionSpec as P

soft_cap = 30.0
norm_eps = 1e-06
tile_rows = 128


def from_behind(block, axis, distance):
    devices = range(lax.axis_size(axis))
    route = [(i - distance, i) for i in devices if i - distance in devices]
    return lax.ppermute(block, axis, route)


def spread(array, axis, root):
    mine = lax.axis_index(axis) == root
    return lax.psum(jnp.where(mine, array, jnp.zeros_like(array)), axis)


def capped(values):
    return soft_cap * jnp.tanh(values / soft_cap)


def normalize(layer_in):
    hidden_f = layer_in.astype(jnp.float32)
    inv_rms = lax.rsqrt(jnp.mean(hidden_f * hidden_f, axis=-1, keepdims=True) + norm_eps)
    return (hidden_f, inv_rms, (hidden_f * inv_rms).astype(jnp.bfloat16))


def gate_probs(normed, ids_now, router_w):
    logits = jnp.dot(normed, router_w, preferred_element_type=jnp.float32)
    one_hot = (
        ids_now[:, :, None] == jnp.arange(router_w.shape[1], dtype=jnp.int32)[None, None, :]
    ).astype(jnp.float32)
    chosen = capped(jnp.sum(one_hot * logits[:, None, :], axis=-1))
    weights = jnp.exp(chosen)
    return (one_hot, chosen, weights / jnp.sum(weights, axis=-1, keepdims=True))


def contract_first(left, right):
    return lax.dot_general(
        left, right, (((0,), (0,)), ((), ())), preferred_element_type=jnp.float32
    )


def contract_last(left, right):
    return lax.dot_general(
        left, right, (((1,), (1,)), ((), ())), preferred_element_type=jnp.float32
    )


def take_slot(stored, micro_at):
    return lax.dynamic_index_in_dim(stored, micro_at, 0, keepdims=False)


def keep_slot(stored, fresh, micro_at, active):
    return lax.dynamic_update_index_in_dim(
        stored, jnp.where(active, fresh, take_slot(stored, micro_at)), micro_at, 0
    )


def placement_rows(ids_now, active, expert_count):
    flat_ids = ids_now.reshape(-1)
    one_hot = (flat_ids[:, None] == jnp.arange(expert_count, dtype=jnp.int32)[None, :]).astype(
        jnp.int32
    )
    one_hot = one_hot * active.astype(jnp.int32)
    before = jnp.cumsum(one_hot, axis=0) - one_hot
    slot_of = jnp.sum(before * one_hot, axis=1)
    counts = jnp.sum(one_hot, axis=0)
    target = jnp.where(active, flat_ids, expert_count)
    return (target, slot_of, counts)


def packing(live_rows, slot_count, buffer_rows):
    offsets = jnp.cumsum(live_rows) - live_rows
    slot_ids = jnp.arange(slot_count, dtype=jnp.int32)
    packed_at = offsets[:, None] + slot_ids[None, :]
    dest_row = jnp.where(slot_ids[None, :] < live_rows[:, None], packed_at, buffer_rows).reshape(-1)
    fetch_row = jnp.minimum(packed_at, buffer_rows - 1).reshape(-1)
    return (dest_row, fetch_row)


def send_tokens(payload, counts):
    return (
        lax.all_to_all(payload, ("expert", "dp"), split_axis=0, concat_axis=0, tiled=True),
        lax.all_to_all(counts, ("expert", "dp"), split_axis=0, concat_axis=0, tiled=True),
    )


def route_rows(payload):
    return lax.all_to_all(payload, ("expert", "dp"), split_axis=0, concat_axis=0, tiled=True)


def expert_forward(packed, gate_w, up_w, down_w):
    gate_act = jnp.dot(packed, gate_w, preferred_element_type=jnp.float32)
    up_act = jnp.dot(packed, up_w, preferred_element_type=jnp.float32)
    hidden_act = (gate_act * jax.nn.sigmoid(gate_act) * up_act).astype(jnp.bfloat16)
    return jnp.dot(hidden_act, down_w, preferred_element_type=jnp.float32).astype(jnp.bfloat16)


def expert_backward(packed, packed_grad, gate_w, up_w, down_w, grad_sums):
    grad_gate, grad_up, grad_down = grad_sums
    gate_act = jnp.dot(packed, gate_w, preferred_element_type=jnp.float32)
    up_act = jnp.dot(packed, up_w, preferred_element_type=jnp.float32)
    sigmoid_gate = jax.nn.sigmoid(gate_act)
    silu_gate = gate_act * sigmoid_gate
    hidden_act = (silu_gate * up_act).astype(jnp.bfloat16)
    grad_down = grad_down + contract_first(hidden_act, packed_grad)
    grad_hidden = contract_last(packed_grad, down_w)
    grad_gate_act = (
        grad_hidden * up_act * sigmoid_gate * (1.0 + gate_act * (1.0 - sigmoid_gate))
    ).astype(jnp.bfloat16)
    grad_up_act = (grad_hidden * silu_gate).astype(jnp.bfloat16)
    grad_gate = grad_gate + contract_first(packed, grad_gate_act)
    grad_up = grad_up + contract_first(packed, grad_up_act)
    results = (contract_last(grad_gate_act, gate_w) + contract_last(grad_up_act, up_w)).astype(
        jnp.bfloat16
    )
    return (grad_gate, grad_up, grad_down, results)


def shards(tokens, expert_ids, labels, router, class_head, w_gate, w_up, w_down):
    section_count = lax.axis_size("section")
    section_index = lax.axis_index("section")
    expert_count = lax.axis_size(("expert", "dp"))
    micro_count, tok_rows, model_width = tokens.shape
    top_count = expert_ids.shape[3]
    slot_count = 2 * tok_rows * top_count // expert_count
    buffer_rows = (expert_count * slot_count + tile_rows - 1) // tile_rows * tile_rows
    route_ids = expert_ids[0]
    router_w = router[0]
    gate_w = w_gate[0, 0]
    up_w = w_up[0, 0]
    down_w = w_down[0, 0]
    hidden_dim = gate_w.shape[1]
    is_last = section_index == section_count - 1
    tick_count = micro_count + section_count - 1
    saved_in = jnp.zeros((micro_count, tok_rows, model_width), jnp.bfloat16)
    saved_out = jnp.zeros((micro_count, tok_rows, top_count, model_width), jnp.bfloat16)
    saved_packed = jnp.zeros((micro_count, buffer_rows, model_width), jnp.bfloat16)
    saved_live = jnp.zeros((micro_count, expert_count), jnp.int32)
    finals = jnp.zeros((micro_count, tok_rows, model_width), jnp.bfloat16)
    incoming = jnp.zeros((tok_rows, model_width), jnp.bfloat16)
    for tick_num in range(tick_count):
        micro_at = tick_num - section_index
        active = (micro_at >= 0) & (micro_at < micro_count)
        micro_at = jnp.clip(micro_at, 0, micro_count - 1)
        layer_in = jnp.where(section_index == 0, take_slot(tokens, micro_at), incoming)
        hidden_f, inv_rms, normed = normalize(layer_in)
        ids_now = take_slot(route_ids, micro_at)
        one_hot, chosen, probs = gate_probs(normed, ids_now, router_w)
        target, slot_of, counts = placement_rows(ids_now, active, expert_count)
        source_rows = jnp.broadcast_to(
            normed[:, None, :], (tok_rows, top_count, model_width)
        ).reshape(-1, model_width)
        outgoing = (
            jnp.zeros((expert_count, slot_count, model_width), jnp.bfloat16)
            .at[target, slot_of]
            .set(source_rows, mode="drop")
        )
        arrived, arrived_counts = send_tokens(
            outgoing, counts.astype(jnp.bfloat16).reshape(expert_count, 1)
        )
        live_rows = arrived_counts[:, 0].astype(jnp.int32)
        dest_row, fetch_row = packing(live_rows, slot_count, buffer_rows)
        packed = (
            jnp.zeros((buffer_rows, model_width), jnp.bfloat16)
            .at[dest_row]
            .set(arrived.reshape(-1, model_width), mode="drop")
        )
        results = expert_forward(packed, gate_w, up_w, down_w)
        returned = route_rows(results[fetch_row].reshape(expert_count, slot_count, model_width))
        expert_out = returned[jnp.minimum(target, expert_count - 1), slot_of].reshape(
            tok_rows, top_count, model_width
        )
        layer_out = (
            hidden_f + jnp.sum(probs[:, :, None] * expert_out.astype(jnp.float32), axis=1)
        ).astype(jnp.bfloat16)
        saved_in = keep_slot(saved_in, layer_in, micro_at, active)
        saved_out = keep_slot(saved_out, expert_out, micro_at, active)
        saved_packed = keep_slot(saved_packed, packed, micro_at, active)
        saved_live = keep_slot(saved_live, live_rows, micro_at, active)
        finals = keep_slot(finals, layer_out, micro_at, active & is_last)
        if tick_num + 1 < tick_count:
            incoming = from_behind(layer_out, "section", 1)
    all_rows = micro_count * tok_rows
    share_rows = all_rows // section_count
    final_all = spread(finals.reshape(-1, model_width), "section", section_count - 1)
    final_rows = lax.dynamic_slice_in_dim(final_all, section_index * share_rows, share_rows, 0)
    label_rows = lax.dynamic_slice_in_dim(
        labels.reshape(-1), section_index * share_rows, share_rows, 0
    )
    class_logits = capped(jnp.dot(final_rows, class_head, preferred_element_type=jnp.float32))
    class_weights = jnp.exp(class_logits)
    class_total = jnp.sum(class_weights, axis=-1, keepdims=True)
    label_hot = (
        label_rows[:, None] == jnp.arange(class_head.shape[1], dtype=jnp.int32)[None, :]
    ).astype(jnp.float32)
    token_loss = jnp.log(class_total[:, 0]) - jnp.sum(label_hot * class_logits, axis=-1)
    scaled = class_logits / soft_cap
    grad_logits = ((class_weights / class_total - label_hot) * (1.0 - scaled * scaled)).astype(
        jnp.bfloat16
    )
    head_term = contract_first(final_rows, grad_logits)
    loss_term = jnp.sum(token_loss)
    top_share = contract_last(grad_logits, class_head).astype(jnp.bfloat16)
    grad_top = lax.all_gather(top_share, "section", axis=0, tiled=True).reshape(
        micro_count, tok_rows, model_width
    )
    grad_gate = jnp.zeros((model_width, hidden_dim), jnp.float32)
    grad_up = jnp.zeros((model_width, hidden_dim), jnp.float32)
    grad_down = jnp.zeros((hidden_dim, model_width), jnp.float32)
    grad_router = jnp.zeros(router_w.shape, jnp.float32)
    incoming_grad = jnp.zeros((tok_rows, model_width), jnp.bfloat16)
    for tick_num in range(tick_count):
        micro_at = micro_count - 1 - tick_num + (section_count - 1 - section_index)
        active = (micro_at >= 0) & (micro_at < micro_count)
        micro_at = jnp.clip(micro_at, 0, micro_count - 1)
        grad_out = jnp.where(is_last, take_slot(grad_top, micro_at), incoming_grad)
        layer_in = take_slot(saved_in, micro_at)
        expert_out = take_slot(saved_out, micro_at)
        hidden_f, inv_rms, normed = normalize(layer_in)
        ids_now = take_slot(route_ids, micro_at)
        one_hot, chosen, probs = gate_probs(normed, ids_now, router_w)
        grad_f = grad_out.astype(jnp.float32)
        grad_prob = jnp.sum(grad_f[:, None, :] * expert_out.astype(jnp.float32), axis=-1)
        grad_rows = (
            (probs[:, :, None] * grad_f[:, None, :]).astype(jnp.bfloat16).reshape(-1, model_width)
        )
        target, slot_of, counts = placement_rows(ids_now, active, expert_count)
        outgoing = (
            jnp.zeros((expert_count, slot_count, model_width), jnp.bfloat16)
            .at[target, slot_of]
            .set(grad_rows, mode="drop")
        )
        arrived = route_rows(outgoing)
        live_rows = take_slot(saved_live, micro_at) * active.astype(jnp.int32)
        dest_row, fetch_row = packing(live_rows, slot_count, buffer_rows)
        packed_grad = (
            jnp.zeros((buffer_rows, model_width), jnp.bfloat16)
            .at[dest_row]
            .set(arrived.reshape(-1, model_width), mode="drop")
        )
        packed_in = jnp.where(
            active, take_slot(saved_packed, micro_at), jnp.zeros((), jnp.bfloat16)
        )
        grad_gate, grad_up, grad_down, results = expert_backward(
            packed_in, packed_grad, gate_w, up_w, down_w, (grad_gate, grad_up, grad_down)
        )
        returned = route_rows(results[fetch_row].reshape(expert_count, slot_count, model_width))
        grad_parts = returned[jnp.minimum(target, expert_count - 1), slot_of].reshape(
            tok_rows, top_count, model_width
        )
        scaled = chosen / soft_cap
        grad_chosen = (
            probs
            * (grad_prob - jnp.sum(probs * grad_prob, axis=-1, keepdims=True))
            * (1.0 - scaled * scaled)
        )
        grad_route = jnp.sum(grad_chosen[:, :, None] * one_hot, axis=1).astype(jnp.bfloat16)
        grad_router = grad_router + jnp.where(active, contract_first(normed, grad_route), 0.0)
        grad_normed = jnp.sum(grad_parts.astype(jnp.float32), axis=1) + contract_last(
            grad_route, router_w
        )
        normed_f = hidden_f * inv_rms
        grad_in = (
            grad_f
            + inv_rms
            * (grad_normed - normed_f * jnp.mean(grad_normed * normed_f, axis=-1, keepdims=True))
        ).astype(jnp.bfloat16)
        if tick_num + 1 < tick_count:
            incoming_grad = from_behind(grad_in, "section", -1)
    head_total, loss_total = lax.psum((head_term, loss_term), ("section", "expert", "dp"))
    router_out = lax.psum(grad_router.astype(jnp.bfloat16), ("expert", "dp")).astype(jnp.float32)[
        None
    ]
    mean_loss = loss_total / (micro_count * tok_rows * expert_count)
    return (
        mean_loss,
        head_total,
        router_out,
        grad_gate.astype(jnp.bfloat16)[None, None],
        grad_up.astype(jnp.bfloat16)[None, None],
        grad_down.astype(jnp.bfloat16)[None, None],
    )


def solution(mesh):
    return jax.shard_map(
        shards,
        mesh=mesh,
        in_specs=(
            P(None, ("expert", "dp"), None),
            P("section", None, ("expert", "dp"), None),
            P(None, ("expert", "dp")),
            P("section", None, None),
            P(),
            P("section", ("expert", "dp"), None, None),
            P("section", ("expert", "dp"), None, None),
            P("section", ("expert", "dp"), None, None),
        ),
        out_specs=(
            P(),
            P(),
            P("section", None, None),
            P("section", ("expert", "dp"), None, None),
            P("section", ("expert", "dp"), None, None),
            P("section", ("expert", "dp"), None, None),
        ),
        check_vma=False,
    )
```

profile of v0, /device:TPU:0, one launch (start us, length us, event | category | flops | bytes accessed | tf_op | source)
XLA Modules:
  0.0 1821.9 jit_solution(11919487635212889691)
XLA Ops:
  24.6 46.2 %scatter_fusion = bf16[8,64,2048]{2,1,0:T(8,128)(2,1)} fusion(bf16[8,64,2048]{2,1,0:T(8,128)(2,1)} %broadcast.1927.clone, s32[256]{0:T(256)S(1)} %bitcast.714, bf16[256,2048]{1,0:T(8,128)(2,1)} %reshape.2808), kind=kCustom, calls=%fused_computation.18 | custom fusion | bytes 3147776 | tf_op jit(solution)/shard_map/scatter | solution.py:162
  79.4 22.4 %all-to-all-done.1 = bf16[8,64,2048]{2,1,0:T(8,128)(2,1)} async-done(((bf16[8,64,2048]{2,1,0:T(8,128)(2,1)}), bf16[8,64,2048]{2,1,0:T(8,128)(2,1)}, u32[]{:S(2)}, u32[]{:S(2)}) %all-to-all-start.1) | async-done | bytes 2097184 | tf_op jit(solution)/shard_map/all_to_all | solution.py:88
  139.3 20.6 %all-to-all-done.2 = bf16[8,64,2048]{2,1,0:T(8,128)(2,1)} async-done(((bf16[8,64,2048]{2,1,0:T(8,128)(2,1)}), bf16[8,64,2048]{2,1,0:T(8,128)(2,1)}, u32[]{:S(2)}, u32[]{:S(2)}) %all-to-all-start.2) | async-done | bytes 2097184 | tf_op jit(solution)/shard_map/all_to_all | solution.py:94
  197.6 46.3 %scatter_fusion.1 = bf16[8,64,2048]{2,1,0:T(8,128)(2,1)} fusion(bf16[8,64,2048]{2,1,0:T(8,128)(2,1)} %broadcast.1927.clone.1, s32[256]{0:T(256)S(1)} %bitcast.718, bf16[256,2048]{1,0:T(8,128)(2,1)} %reshape.2822), kind=kCustom, calls=%fused_computation.20 | custom fusion | bytes 3147776 | tf_op jit(solution)/shard_map/scatter | solution.py:162
  259.1 24.3 %all-to-all-done.4 = bf16[8,64,2048]{2,1,0:T(8,128)(2,1)} async-done(((bf16[8,64,2048]{2,1,0:T(8,128)(2,1)}), bf16[8,64,2048]{2,1,0:T(8,128)(2,1)}, u32[]{:S(2)}, u32[]{:S(2)}) %all-to-all-start.4) | async-done | bytes 2097184 | tf_op jit(solution)/shard_map/all_to_all | solution.py:88
  321.8 23.0 %all-to-all-done.5 = bf16[8,64,2048]{2,1,0:T(8,128)(2,1)} async-done(((bf16[8,64,2048]{2,1,0:T(8,128)(2,1)}), bf16[8,64,2048]{2,1,0:T(8,128)(2,1)}, u32[]{:S(2)}, u32[]{:S(2)}) %all-to-all-start.5) | async-done | bytes 2097184 | tf_op jit(solution)/shard_map/all_to_all | solution.py:94
  379.1 40.3 %scatter_fusion.2 = bf16[8,64,2048]{2,1,0:T(8,128)(2,1)} fusion(bf16[8,64,2048]{2,1,0:T(8,128)(2,1)} %broadcast.1927.clone.2, s32[256]{0:T(256)S(1)} %bitcast.722, bf16[256,2048]{1,0:T(8,128)(2,1)} %reshape.2836), kind=kCustom, calls=%fused_computation.22 | custom fusion | bytes 3147776 | tf_op jit(solution)/shard_map/scatter | solution.py:162
  424.4 26.0 %all-to-all-done.7 = bf16[8,64,2048]{2,1,0:T(8,128)(2,1)} async-done(((bf16[8,64,2048]{2,1,0:T(8,128)(2,1)}), bf16[8,64,2048]{2,1,0:T(8,128)(2,1)}, u32[]{:S(2)}, u32[]{:S(2)}) %all-to-all-start.7) | async-done | bytes 2097184 | tf_op jit(solution)/shard_map/all_to_all | solution.py:88
  486.4 22.6 %all-to-all-done.8 = bf16[8,64,2048]{2,1,0:T(8,128)(2,1)} async-done(((bf16[8,64,2048]{2,1,0:T(8,128)(2,1)}), bf16[8,64,2048]{2,1,0:T(8,128)(2,1)}, u32[]{:S(2)}, u32[]{:S(2)}) %all-to-all-start.8) | async-done | bytes 2097184 | tf_op jit(solution)/shard_map/all_to_all | solution.py:94
  544.9 46.4 %scatter_fusion.3 = bf16[8,64,2048]{2,1,0:T(8,128)(2,1)} fusion(bf16[8,64,2048]{2,1,0:T(8,128)(2,1)} %broadcast.1927.clone.3, s32[256]{0:T(256)S(1)} %bitcast.726, bf16[256,2048]{1,0:T(8,128)(2,1)} %reshape.2850), kind=kCustom, calls=%fused_computation.24 | custom fusion | bytes 3147776 | tf_op jit(solution)/shard_map/scatter | solution.py:162
  603.3 19.1 %all-to-all-done.10 = bf16[8,64,2048]{2,1,0:T(8,128)(2,1)} async-done(((bf16[8,64,2048]{2,1,0:T(8,128)(2,1)}), bf16[8,64,2048]{2,1,0:T(8,128)(2,1)}, u32[]{:S(2)}, u32[]{:S(2)}) %all-to-all-start.10) | async-done | bytes 2097184 | tf_op jit(solution)/shard_map/all_to_all | solution.py:88
  720.5 40.3 %scatter_fusion.4 = bf16[8,64,2048]{2,1,0:T(8,128)(2,1)} fusion(bf16[8,64,2048]{2,1,0:T(8,128)(2,1)} %broadcast.1927.clone.4, s32[256]{0:T(256)S(1)} %bitcast.730, bf16[256,2048]{1,0:T(8,128)(2,1)} %reshape.2864), kind=kCustom, calls=%fused_computation.26 | custom fusion | bytes 3147776 | tf_op jit(solution)/shard_map/scatter | solution.py:162
  831.1 18.8 %all-to-all-done.14 = bf16[8,64,2048]{2,1,0:T(8,128)(2,1)} async-done(((bf16[8,64,2048]{2,1,0:T(8,128)(2,1)}), bf16[8,64,2048]{2,1,0:T(8,128)(2,1)}, u32[]{:S(2)}, u32[]{:S(2)}) %all-to-all-start.14) | async-done | bytes 2097184 | tf_op jit(solution)/shard_map/all_to_all | solution.py:94
  876.1 29.6 %all-reduce.3.cloned.1.call-done = bf16[128,2048]{1,0:T(8,128)(2,1)} async-done(((bf16[128,2048]{1,0:T(8,128)(2,1)}), bf16[128,2048]{1,0:T(8,128)(2,1)}) %all-reduce.3.cloned.1.call-update) | async-done | bytes 524304 | tf_op jit(solution)/shard_map/psum | solution.py:19
  937.8 40.3 %scatter_fusion.5 = bf16[8,64,2048]{2,1,0:T(8,128)(2,1)} fusion(bf16[8,64,2048]{2,1,0:T(8,128)(2,1)} %broadcast.1927.clone.5, s32[256]{0:T(256)S(1)} %bitcast.731, bf16[256,2048]{1,0:T(8,128)(2,1)} %multiply_convert_fusion.4), kind=kCustom, calls=%fused_computation.28 | custom fusion | bytes 3147776 | tf_op jit(solution)/shard_map/scatter | solution.py:237
  1042.0 26.6 %all-to-all-done.16 = bf16[8,64,2048]{2,1,0:T(8,128)(2,1)} async-done(((bf16[8,64,2048]{2,1,0:T(8,128)(2,1)}), bf16[8,64,2048]{2,1,0:T(8,128)(2,1)}, u32[]{:S(2)}, u32[]{:S(2)}) %all-to-all-start.16) | async-done | bytes 2097184 | tf_op jit(solution)/shard_map/all_to_all | solution.py:94
  1110.9 40.3 %scatter_fusion.6 = bf16[8,64,2048]{2,1,0:T(8,128)(2,1)} fusion(bf16[8,64,2048]{2,1,0:T(8,128)(2,1)} %broadcast.1927.clone.6, s32[256]{0:T(256)S(1)} %bitcast.727, bf16[256,2048]{1,0:T(8,128)(2,1)} %multiply_convert_fusion.3), kind=kCustom, calls=%fused_computation.30 | custom fusion | bytes 3147776 | tf_op jit(solution)/shard_map/scatter | solution.py:237
  1161.5 21.0 %all-to-all-done.17 = bf16[8,64,2048]{2,1,0:T(8,128)(2,1)} async-done(((bf16[8,64,2048]{2,1,0:T(8,128)(2,1)}), bf16[8,64,2048]{2,1,0:T(8,128)(2,1)}, u32[]{:S(2)}, u32[]{:S(2)}) %all-to-all-start.17) | async-done | bytes 2097184 | tf_op jit(solution)/shard_map/all_to_all | solution.py:94
  1215.5 26.4 %all-to-all-done.18 = bf16[8,64,2048]{2,1,0:T(8,128)(2,1)} async-done(((bf16[8,64,2048]{2,1,0:T(8,128)(2,1)}), bf16[8,64,2048]{2,1,0:T(8,128)(2,1)}, u32[]{:S(2)}, u32[]{:S(2)}) %all-to-all-start.18) | async-done | bytes 2097184 | tf_op jit(solution)/shard_map/all_to_all | solution.py:94
  1284.3 40.3 %scatter_fusion.7 = bf16[8,64,2048]{2,1,0:T(8,128)(2,1)} fusion(bf16[8,64,2048]{2,1,0:T(8,128)(2,1)} %broadcast.1927.clone.7, s32[256]{0:T(256)S(1)} %bitcast.723, bf16[256,2048]{1,0:T(8,128)(2,1)} %multiply_convert_fusion.2), kind=kCustom, calls=%fused_computation.32 | custom fusion | bytes 3147776 | tf_op jit(solution)/shard_map/scatter | solution.py:237
  1350.5 45.9 %psum.29 = f32[]{:T(128)} all-reduce(f32[]{:T(128)} %subtract_reduce_fusion), channel_id=1, replica_groups=mesh['section'=4,'expert'=4,'dp'=2] {'section','expert','dp'}, use_global_device_ids=true, to_apply=%region_59.60 | all-reduce | flops 1 | bytes 8 | tf_op jit(solution)/shard_map/psum | solution.py:276
  1500.2 46.2 %scatter_fusion.8 = bf16[8,64,2048]{2,1,0:T(8,128)(2,1)} fusion(bf16[8,64,2048]{2,1,0:T(8,128)(2,1)} %broadcast.1927.clone.8, s32[256]{0:T(256)S(1)} %bitcast.719, bf16[256,2048]{1,0:T(8,128)(2,1)} %multiply_convert_fusion.1), kind=kCustom, calls=%fused_computation.34 | custom fusion | bytes 3147776 | tf_op jit(solution)/shard_map/scatter | solution.py:237
  1671.0 46.3 %scatter_fusion.9 = bf16[8,64,2048]{2,1,0:T(8,128)(2,1)} fusion(bf16[8,64,2048]{2,1,0:T(8,128)(2,1)} %broadcast.1927, s32[256]{0:T(256)S(1)} %bitcast.715, bf16[256,2048]{1,0:T(8,128)(2,1)} %multiply_convert_fusion), kind=kCustom, calls=%fused_computation.36 | custom fusion | bytes 3147776 | tf_op jit(solution)/shard_map/scatter | solution.py:237
  1739.9 25.2 %psum.31 = bf16[1,2048,8]{1,2,0:T(8,128)(2,1)S(1)} all-reduce(bf16[1,2048,8]{1,2,0:T(8,128)(2,1)S(1)} %fusion.107), channel_id=1, replica_groups=mesh['section'=4,'expert'=4,'dp'=2] {'expert','dp'}, use_global_device_ids=true, to_apply=%region_111.112 | all-reduce | flops 16384 | bytes 65536 | tf_op jit(solution)/shard_map/psum | solution.py:277
  (694 shorter events, 1019.4 us)
Async XLA Ops:
  10.2 60.6 %all-to-all-start = ((bf16[8,1,1]{2,1,0:T(2,128)(2,1)}), bf16[8,1,1]{2,1,0:T(2,128)(2,1)S(1)}, u32[]{:S(2)}, u32[]{:S(2)}) async-start(bf16[8,1,1]{2,1,0:T(2,128)(2,1)} %copy.156), calls=%async_computation | async-start | bytes 8192 | tf_op jit(solution)/shard_map/all_to_all | solution.py:89
  70.8 31.0 %all-to-all-start.1 = ((bf16[8,64,2048]{2,1,0:T(8,128)(2,1)}), bf16[8,64,2048]{2,1,0:T(8,128)(2,1)}, u32[]{:S(2)}, u32[]{:S(2)}) async-start(bf16[8,64,2048]{2,1,0:T(8,128)(2,1)} %scatter_fusion), calls=%async_computation.1 | async-start | bytes 4194304 | tf_op jit(solution)/shard_map/all_to_all | solution.py:88
  128.9 31.0 %all-to-all-start.2 = ((bf16[8,64,2048]{2,1,0:T(8,128)(2,1)}), bf16[8,64,2048]{2,1,0:T(8,128)(2,1)}, u32[]{:S(2)}, u32[]{:S(2)}) async-start(bf16[8,64,2048]{2,1,0:T(8,128)(2,1)} %bitcast.739), calls=%async_computation.2 | async-start | bytes 4194304 | tf_op jit(solution)/shard_map/all_to_all | solution.py:94
  159.9 83.9 %all-to-all-start.3 = ((bf16[8,1,1]{2,1,0:T(2,128)(2,1)}), bf16[8,1,1]{2,1,0:T(2,128)(2,1)S(1)}, u32[]{:S(2)}, u32[]{:S(2)}) async-start(bf16[8,1,1]{2,1,0:T(2,128)(2,1)} %copy.161), calls=%async_computation.3 | async-start | bytes 8192 | tf_op jit(solution)/shard_map/all_to_all | solution.py:89
  252.3 31.1 %all-to-all-start.4 = ((bf16[8,64,2048]{2,1,0:T(8,128)(2,1)}), bf16[8,64,2048]{2,1,0:T(8,128)(2,1)}, u32[]{:S(2)}, u32[]{:S(2)}) async-start(bf16[8,64,2048]{2,1,0:T(8,128)(2,1)} %scatter_fusion.1), calls=%async_computation.4 | async-start | bytes 4194304 | tf_op jit(solution)/shard_map/all_to_all | solution.py:88
  283.4 30.5 %all-to-all-start.9 = ((bf16[8,1,1]{2,1,0:T(2,128)(2,1)}), bf16[8,1,1]{2,1,0:T(2,128)(2,1)S(1)}, u32[]{:S(2)}, u32[]{:S(2)}) async-start(bf16[8,1,1]{2,1,0:T(2,128)(2,1)} %copy.171), calls=%async_computation.9 | async-start | bytes 8192 | tf_op jit(solution)/shard_map/all_to_all | solution.py:89
  313.8 31.0 %all-to-all-start.5 = ((bf16[8,64,2048]{2,1,0:T(8,128)(2,1)}), bf16[8,64,2048]{2,1,0:T(8,128)(2,1)}, u32[]{:S(2)}, u32[]{:S(2)}) async-start(bf16[8,64,2048]{2,1,0:T(8,128)(2,1)} %bitcast.740), calls=%async_computation.5 | async-start | bytes 4194304 | tf_op jit(solution)/shard_map/all_to_all | solution.py:94
  419.4 31.0 %all-to-all-start.7 = ((bf16[8,64,2048]{2,1,0:T(8,128)(2,1)}), bf16[8,64,2048]{2,1,0:T(8,128)(2,1)}, u32[]{:S(2)}, u32[]{:S(2)}) async-start(bf16[8,64,2048]{2,1,0:T(8,128)(2,1)} %scatter_fusion.2), calls=%async_computation.7 | async-start | bytes 4194304 | tf_op jit(solution)/shard_map/all_to_all | solution.py:88
  477.9 31.2 %all-to-all-start.8 = ((bf16[8,64,2048]{2,1,0:T(8,128)(2,1)}), bf16[8,64,2048]{2,1,0:T(8,128)(2,1)}, u32[]{:S(2)}, u32[]{:S(2)}) async-start(bf16[8,64,2048]{2,1,0:T(8,128)(2,1)} %bitcast.741), calls=%async_computation.8 | async-start | bytes 4194304 | tf_op jit(solution)/shard_map/all_to_all | solution.py:94
  591.3 31.0 %all-to-all-start.10 = ((bf16[8,64,2048]{2,1,0:T(8,128)(2,1)}), bf16[8,64,2048]{2,1,0:T(8,128)(2,1)}, u32[]{:S(2)}, u32[]{:S(2)}) async-start(bf16[8,64,2048]{2,1,0:T(8,128)(2,1)} %scatter_fusion.3), calls=%async_computation.10 | async-start | bytes 4194304 | tf_op jit(solution)/shard_map/all_to_all | solution.py:88
  649.5 31.4 %all-to-all-start.11 = ((bf16[8,64,2048]{2,1,0:T(8,128)(2,1)}), bf16[8,64,2048]{2,1,0:T(8,128)(2,1)}, u32[]{:S(2)}, u32[]{:S(2)}) async-start(bf16[8,64,2048]{2,1,0:T(8,128)(2,1)} %bitcast.744), calls=%async_computation.11 | async-start | bytes 4194304 | tf_op jit(solution)/shard_map/all_to_all | solution.py:94
  760.8 31.2 %all-to-all-start.13 = ((bf16[8,64,2048]{2,1,0:T(8,128)(2,1)}), bf16[8,64,2048]{2,1,0:T(8,128)(2,1)}, u32[]{:S(2)}, u32[]{:S(2)}) async-start(bf16[8,64,2048]{2,1,0:T(8,128)(2,1)} %scatter_fusion.4), calls=%async_computation.13 | async-start | bytes 4194304 | tf_op jit(solution)/shard_map/all_to_all | solution.py:88
  819.0 31.0 %all-to-all-start.14 = ((bf16[8,64,2048]{2,1,0:T(8,128)(2,1)}), bf16[8,64,2048]{2,1,0:T(8,128)(2,1)}, u32[]{:S(2)}, u32[]{:S(2)}) async-start(bf16[8,64,2048]{2,1,0:T(8,128)(2,1)} %bitcast.743), calls=%async_computation.14 | async-start | bytes 4194304 | tf_op jit(solution)/shard_map/all_to_all | solution.py:94
  823.3 82.4 %all-reduce.3.cloned.1.call-start = ((), (), s32[]{:S(2)}) async-start(), calls=%async_computation.24 | async-start | bytes 1048576 | tf_op jit(solution)/shard_map/psum | solution.py:19
  978.1 31.4 %all-to-all-start.15 = ((bf16[8,64,2048]{2,1,0:T(8,128)(2,1)}), bf16[8,64,2048]{2,1,0:T(8,128)(2,1)}, u32[]{:S(2)}, u32[]{:S(2)}) async-start(bf16[8,64,2048]{2,1,0:T(8,128)(2,1)} %scatter_fusion.5), calls=%async_computation.15 | async-start | bytes 4194304 | tf_op jit(solution)/shard_map/all_to_all | solution.py:94
  1037.4 31.2 %all-to-all-start.16 = ((bf16[8,64,2048]{2,1,0:T(8,128)(2,1)}), bf16[8,64,2048]{2,1,0:T(8,128)(2,1)}, u32[]{:S(2)}, u32[]{:S(2)}) async-start(bf16[8,64,2048]{2,1,0:T(8,128)(2,1)} %bitcast.747), calls=%async_computation.16 | async-start | bytes 4194304 | tf_op jit(solution)/shard_map/all_to_all | solution.py:94
  1151.2 31.2 %all-to-all-start.17 = ((bf16[8,64,2048]{2,1,0:T(8,128)(2,1)}), bf16[8,64,2048]{2,1,0:T(8,128)(2,1)}, u32[]{:S(2)}, u32[]{:S(2)}) async-start(bf16[8,64,2048]{2,1,0:T(8,128)(2,1)} %scatter_fusion.6), calls=%async_computation.17 | async-start | bytes 4194304 | tf_op jit(solution)/shard_map/all_to_all | solution.py:94
  1210.8 31.1 %all-to-all-start.18 = ((bf16[8,64,2048]{2,1,0:T(8,128)(2,1)}), bf16[8,64,2048]{2,1,0:T(8,128)(2,1)}, u32[]{:S(2)}, u32[]{:S(2)}) async-start(bf16[8,64,2048]{2,1,0:T(8,128)(2,1)} %bitcast.742), calls=%async_computation.18 | async-start | bytes 4194304 | tf_op jit(solution)/shard_map/all_to_all | solution.py:94
  1324.6 72.4 %all-to-all-start.19 = ((bf16[8,64,2048]{2,1,0:T(8,128)(2,1)}), bf16[8,64,2048]{2,1,0:T(8,128)(2,1)}, u32[]{:S(2)}, u32[]{:S(2)}) async-start(bf16[8,64,2048]{2,1,0:T(8,128)(2,1)} %scatter_fusion.7), calls=%async_computation.19 | async-start | bytes 4194304 | tf_op jit(solution)/shard_map/all_to_all | solution.py:94
  1329.0 482.2 %all-reduce.5.cloned.1.call-start = ((), (), s32[]{:S(2)}) async-start(), calls=%async_computation.25 | async-start | bytes 2097152 | tf_op jit(solution)/shard_map/psum | solution.py:276
  1425.4 32.1 %all-to-all-start.20 = ((bf16[8,64,2048]{2,1,0:T(8,128)(2,1)}), bf16[8,64,2048]{2,1,0:T(8,128)(2,1)}, u32[]{:S(2)}, u32[]{:S(2)}) async-start(bf16[8,64,2048]{2,1,0:T(8,128)(2,1)} %bitcast.745), calls=%async_computation.20 | async-start | bytes 4194304 | tf_op jit(solution)/shard_map/all_to_all | solution.py:94
  1546.4 31.0 %all-to-all-start.21 = ((bf16[8,64,2048]{2,1,0:T(8,128)(2,1)}), bf16[8,64,2048]{2,1,0:T(8,128)(2,1)}, u32[]{:S(2)}, u32[]{:S(2)}) async-start(bf16[8,64,2048]{2,1,0:T(8,128)(2,1)} %scatter_fusion.8), calls=%async_computation.21 | async-start | bytes 4194304 | tf_op jit(solution)/shard_map/all_to_all | solution.py:94
  1605.6 31.2 %all-to-all-start.22 = ((bf16[8,64,2048]{2,1,0:T(8,128)(2,1)}), bf16[8,64,2048]{2,1,0:T(8,128)(2,1)}, u32[]{:S(2)}, u32[]{:S(2)}) async-start(bf16[8,64,2048]{2,1,0:T(8,128)(2,1)} %bitcast.746), calls=%async_computation.22 | async-start | bytes 4194304 | tf_op jit(solution)/shard_map/all_to_all | solution.py:94
  1717.3 48.4 %all-to-all-start.23 = ((bf16[8,64,2048]{2,1,0:T(8,128)(2,1)}), bf16[8,64,2048]{2,1,0:T(8,128)(2,1)}, u32[]{:S(2)}, u32[]{:S(2)}) async-start(bf16[8,64,2048]{2,1,0:T(8,128)(2,1)} %scatter_fusion.9), calls=%async_computation.23 | async-start | bytes 4194304 | tf_op jit(solution)/shard_map/all_to_all | solution.py:94
  (100 other events, 2341.0 us)
Sparse Core Ops, SparseCore 0:
  870.8 34.8 all-reduce.2
  1350.6 137.3 all-reduce.4
where the time goes:
time: 1850 us; the launch traced here: 1820 us
  local copies, waits for them, and re-layouts  799 us (43%)
  waiting for transfers between devices  373 us (20%)
  matrix products  290 us (16%)
  starting transfers between devices  127 us (7%)
  other arithmetic  120 us (6%)
  blocking collectives  95.2 us (5%)
    scatter x10, local copies, waits for them, and re-layouts, shards(): outgoing = jnp.zeros((expert_count, slot_count, model_width), jnp.bfloat1...  433 us
    all_to_all x14, waiting for transfers between devices, route_rows(): lax.all_to_all(payload, ('expert', 'dp'), split_axis=0, concat_axis=0, ti...  210 us
    dot_general x21, matrix products, contract_first(): lax.dot_general(left, right, (((0,), (0,)), ((), ())), preferred_element_...  111 us
    all_to_all x5, waiting for transfers between devices, send_tokens(): lax.all_to_all(payload, ('expert', 'dp'), split_axis=0, concat_axis=0, ti...  100 us
    gather x9, local copies, waits for them, and re-layouts, shards(): returned[jnp.minimum(target, expert_count - 1), slot_of]  94.2 us
    gather x9, local copies, waits for them, and re-layouts, shards(): results[fetch_row].reshape(expert_count, slot_count, model_width)  64 us
    all_to_all x14, starting transfers between devices, route_rows(): lax.all_to_all(payload, ('expert', 'dp'), split_axis=0, concat_axis=0, ti...  63.1 us
    dot_general x18, matrix products, contract_last(): lax.dot_general(left, right, (((1,), (1,)), ((), ())), preferred_element_...  50.6 us
  transfers between devices with their start and end apart: 33, of which 25 were waited for; matrix products, arithmetic and copies ran while one was open for 34% of the time, Pallas kernels for 0%

commit v1 on v0

v1 whole, which is shorter than its diff:
```python
import functools

import jax
import jax.numpy as jnp
from jax import lax
from jax.experimental import pallas as pl
from jax.experimental.pallas import tpu as pltpu
from jax.sharding import PartitionSpec as P

soft_cap = 30.0
norm_eps = 1e-06
lanes = 128
MESH = pl.DeviceIdType.MESH
group = ("expert", "dp")


def capped(values):
    return soft_cap * jnp.tanh(values / soft_cap)


def dot_plain(left, right):
    return jnp.dot(left, right, preferred_element_type=jnp.float32)


def contract_first(left, right):
    return lax.dot_general(
        left, right, (((0,), (0,)), ((), ())), preferred_element_type=jnp.float32
    )


def contract_last(left, right):
    return lax.dot_general(
        left, right, (((1,), (1,)), ((), ())), preferred_element_type=jnp.float32
    )


def relay_kernel(sizes, chunks, step, first, carried_ref, root_ref, out_ref,
                 z_send, z_recv, own_sem, x_send, x_recv, d_send, d_recv, f_send, f_recv):
    sections, experts, cores = sizes
    s, e, d = lax.axis_index("section"), lax.axis_index("expert"), lax.axis_index("dp")
    last = sections - 1 - first
    me = e * cores + d
    rows = carried_ref.shape[0] // chunks

    barrier = pltpu.get_barrier_semaphore()
    for off in range(1, experts):
        pl.semaphore_signal(barrier, inc=1, device_id={"expert": lax.rem(e + off, experts)}, device_id_type=MESH)
    for off in range(1, cores):
        pl.semaphore_signal(barrier, inc=1, device_id={"dp": lax.rem(d + off, cores)}, device_id_type=MESH)

    @pl.when(s != first)
    def _():
        pl.semaphore_signal(barrier, inc=1, device_id={"section": s - step}, device_id_type=MESH)

    pl.semaphore_wait(barrier, experts + cores - 2 + (s != last).astype(jnp.int32))

    def part(c):
        return pl.ds(c * rows, rows)

    def shift(c):
        return pltpu.make_async_remote_copy(
            src_ref=carried_ref.at[part(c)], dst_ref=out_ref.at[me, part(c)],
            send_sem=z_send.at[c], recv_sem=z_recv.at[c],
            device_id={"section": lax.rem(s + step + sections, sections)}, device_id_type=MESH)

    def local(c):
        return pltpu.make_async_copy(root_ref.at[part(c)], out_ref.at[me, part(c)], own_sem.at[c])

    def across(c, off):
        return pltpu.make_async_remote_copy(
            src_ref=out_ref.at[me, part(c)], dst_ref=out_ref.at[me, part(c)],
            send_sem=x_send.at[c, off - 1], recv_sem=x_recv.at[c, off - 1],
            device_id={"expert": lax.rem(e + off, experts)}, device_id_type=MESH)

    def beside(c, off):
        return pltpu.make_async_remote_copy(
            src_ref=out_ref.at[me, part(c)], dst_ref=out_ref.at[me, part(c)],
            send_sem=d_send.at[c, off - 1], recv_sem=d_recv.at[c, off - 1],
            device_id={"dp": lax.rem(d + off, cores)}, device_id_type=MESH)

    def onward(c, off, far):
        source = lax.rem(e - far + experts, experts) * cores + d
        return pltpu.make_async_remote_copy(
            src_ref=out_ref.at[source, part(c)], dst_ref=out_ref.at[source, part(c)],
            send_sem=f_send.at[c, off - 1, far - 1], recv_sem=f_recv.at[c, off - 1, far - 1],
            device_id={"dp": lax.rem(d + off, cores)}, device_id_type=MESH)

    @pl.when(s != last)
    def _():
        for c in range(chunks):
            shift(c).start()

    @pl.when(s == first)
    def _():
        for c in range(chunks):
            local(c).start()

    for c in range(chunks):
        @pl.when(s == first)
        def _():
            local(c).wait()

        @pl.when(s != first)
        def _():
            shift(c).wait_recv()

        for off in range(1, experts):
            across(c, off).start()
        for off in range(1, cores):
            beside(c, off).start()
    for c in range(chunks):
        for far in range(1, experts):
            across(c, far).wait_recv()
            for off in range(1, cores):
                onward(c, off, far).start()
    for c in range(chunks):
        for off in range(1, cores):
            beside(c, off).wait()
            for far in range(1, experts):
                onward(c, off, far).wait()
        for off in range(1, experts):
            across(c, off).wait_send()

    @pl.when(s != last)
    def _():
        for c in range(chunks):
            shift(c).wait_send()


def relay(sizes, carried, root, step, first, call_id):
    sections, experts, cores = sizes
    rows, width = carried.shape
    chunks = 4 if rows % 64 == 0 else 1
    dma = pltpu.SemaphoreType.DMA
    out = pl.pallas_call(
        functools.partial(relay_kernel, sizes, chunks, step, first),
        out_shape=jax.ShapeDtypeStruct((experts * cores, rows, width), carried.dtype),
        in_specs=[pl.BlockSpec(memory_space=pltpu.VMEM)] * 2,
        out_specs=pl.BlockSpec(memory_space=pltpu.VMEM),
        scratch_shapes=[
            dma((chunks,)), dma((chunks,)), dma((chunks,)),
            dma((chunks, experts - 1)), dma((chunks, experts - 1)),
            dma((chunks, cores - 1)), dma((chunks, cores - 1)),
            dma((chunks, cores - 1, experts - 1)), dma((chunks, cores - 1, experts - 1)),
        ],
        compiler_params=pltpu.CompilerParams(collective_id=call_id, has_side_effects=True),
    )(carried, root)
    return out.reshape(experts * cores * rows, width)


def give_back_kernel(sizes, parts_ref, out_ref, own_sem, send_sem, recv_sem):
    sections, experts, cores = sizes
    e, d = lax.axis_index("expert"), lax.axis_index("dp")
    me = e * cores + d
    peers = [(x, c) for x in range(experts) for c in range(cores) if (x, c) != (0, 0)]

    def place(x, c):
        return lax.rem(e + x, experts), lax.rem(d + c, cores)

    barrier = pltpu.get_barrier_semaphore()
    for x, c in peers:
        to_e, to_d = place(x, c)
        pl.semaphore_signal(barrier, inc=1, device_id={"expert": to_e, "dp": to_d}, device_id_type=MESH)
    pl.semaphore_wait(barrier, len(peers))
    own = pltpu.make_async_copy(parts_ref.at[me], out_ref.at[me], own_sem)
    copies = []
    for n, (x, c) in enumerate(peers):
        to_e, to_d = place(x, c)
        copies.append(pltpu.make_async_remote_copy(
            src_ref=parts_ref.at[to_e * cores + to_d], dst_ref=out_ref.at[me],
            send_sem=send_sem.at[n], recv_sem=recv_sem.at[n],
            device_id={"expert": to_e, "dp": to_d}, device_id_type=MESH))
    for copy in copies:
        copy.start()
    own.start()
    own.wait()
    for copy in copies:
        copy.wait()


def give_back(sizes, parts, call_id):
    sections, experts, cores = sizes
    count = experts * cores
    dma = pltpu.SemaphoreType.DMA
    parts = parts.reshape(count, parts.shape[0] // count, parts.shape[1])
    return pl.pallas_call(
        functools.partial(give_back_kernel, sizes),
        out_shape=jax.ShapeDtypeStruct(parts.shape, parts.dtype),
        in_specs=[pl.BlockSpec(memory_space=pltpu.VMEM)],
        out_specs=pl.BlockSpec(memory_space=pltpu.VMEM),
        scratch_shapes=[dma(()), dma((count - 1,)), dma((count - 1,))],
        compiler_params=pltpu.CompilerParams(collective_id=call_id, has_side_effects=True),
    )(parts)


def shards(sizes, tokens, expert_ids, labels, router, class_head, w_gate, w_up, w_down):
    sections, experts, cores = sizes
    s = lax.axis_index("section")
    me = lax.axis_index("expert") * cores + lax.axis_index("dp")
    micro_count, tok_rows, width = tokens.shape
    router_w = router[0]
    router_t = router_w.T
    expert_count = router_w.shape[1]
    gate_w, up_w, down_w = w_gate[0, 0], w_up[0, 0], w_down[0, 0]
    hidden_dim = gate_w.shape[1]
    extra = (expert_count + lanes - 1) // lanes * lanes
    both_w = jnp.concatenate(
        [gate_w, up_w, jnp.pad(router_w, ((0, 0), (0, extra - expert_count)))], axis=1)
    is_last = s == sections - 1
    ticks = micro_count + sections - 1

    ids_all = lax.all_gather(expert_ids[0], group, axis=1, tiled=True)
    picks = jnp.transpose(ids_all, (0, 2, 1))
    named = jnp.arange(expert_count, dtype=jnp.int32)
    masks = jnp.any(picks[:, :, None, :] == named[None, None, :, None], axis=1).astype(jnp.float32)

    def own(rows_all):
        return lax.dynamic_slice_in_dim(rows_all, me * tok_rows, tok_rows, 0)

    kept = []
    finals = []
    layer_out = jnp.zeros((tok_rows, width), jnp.bfloat16)
    for t in range(ticks):
        hidden_all = relay(sizes, layer_out, tokens[min(t, micro_count - 1)], 1, 0, 0)
        mask = lax.dynamic_index_in_dim(masks, jnp.clip(t - s, 0, micro_count - 1), 0, keepdims=False)
        hidden_f = hidden_all.astype(jnp.float32)
        inv_rms = lax.rsqrt(jnp.mean(hidden_f * hidden_f, axis=-1, keepdims=True) + norm_eps)
        normed = (hidden_f * inv_rms).astype(jnp.bfloat16)
        chosen = capped(contract_last(router_t, normed))
        weights = jnp.exp(chosen) * mask
        probs = weights / jnp.sum(weights, axis=0, keepdims=True)
        scaled = chosen / soft_cap
        slope = probs * (1.0 - scaled * scaled)
        mine = lax.dynamic_index_in_dim(probs, me, 0, keepdims=False)[:, None]
        gate_up = dot_plain(normed, both_w[:, : 2 * hidden_dim])
        gate_act, up_act = gate_up[:, :hidden_dim], gate_up[:, hidden_dim:]
        sig = jax.nn.sigmoid(gate_act)
        silu = gate_act * sig
        hidden_w = (mine * silu * up_act).astype(jnp.bfloat16)
        d_gate = (mine * up_act * sig * (1.0 + gate_act * (1.0 - sig))).astype(jnp.bfloat16)
        d_up = (mine * silu).astype(jnp.bfloat16)
        partial = dot_plain(hidden_w, down_w).astype(jnp.bfloat16)
        mix = jnp.sum(give_back(sizes, partial, 1).astype(jnp.float32), axis=0)
        layer_in = own(hidden_all)
        layer_out = (layer_in.astype(jnp.float32) + mix).astype(jnp.bfloat16)
        kept.append((layer_in, mix, normed, chosen, slope, hidden_w, d_gate, d_up))
        if t >= sections - 1:
            finals.append(layer_out)

    final_rows = jnp.concatenate(finals, axis=0)
    class_logits = capped(dot_plain(final_rows, class_head))
    class_weights = jnp.exp(class_logits)
    class_total = jnp.sum(class_weights, axis=-1, keepdims=True)
    label_hot = (
        labels.reshape(-1)[:, None] == jnp.arange(class_head.shape[1], dtype=jnp.int32)[None, :]
    ).astype(jnp.float32)
    token_loss = jnp.log(class_total[:, 0]) - jnp.sum(label_hot * class_logits, axis=-1)
    scaled = class_logits / soft_cap
    grad_logits = ((class_weights / class_total - label_hot) * (1.0 - scaled * scaled)).astype(
        jnp.bfloat16
    )
    head_term = jnp.where(is_last, contract_first(final_rows, grad_logits), 0.0)
    loss_term = jnp.where(is_last, jnp.sum(token_loss), 0.0)
    grad_top = contract_last(grad_logits, class_head).astype(jnp.bfloat16)
    grad_top = grad_top.reshape(micro_count, tok_rows, width)
    head_total, loss_total = lax.psum((head_term, loss_term), ("section",) + group)

    grads = [None] * ticks
    grad_in = jnp.zeros((tok_rows, width), jnp.bfloat16)
    for u in range(ticks):
        t = ticks - 1 - u
        layer_in, mix, normed, chosen, slope, hidden_w, d_gate, d_up = kept[t]
        grad_all = relay(
            sizes, grad_in, grad_top[max(micro_count - 1 - u, 0)], -1, sections - 1, 2)
        down_grad = contract_last(grad_all, down_w)
        grad_acts = jnp.concatenate(
            [(down_grad * d_gate).astype(jnp.bfloat16), (down_grad * d_up).astype(jnp.bfloat16)],
            axis=1)
        my_scaled = lax.dynamic_index_in_dim(chosen, me, 0, keepdims=False) / soft_cap
        gain = jnp.sum(down_grad * hidden_w.astype(jnp.float32), axis=-1) * (1.0 - my_scaled * my_scaled)
        route = jnp.where(
            jnp.arange(extra, dtype=jnp.int32)[None, :] == me, gain[:, None], 0.0
        ).astype(jnp.bfloat16)
        grad_f = own(grad_all).astype(jnp.float32)
        shared = jnp.sum(grad_f * mix, axis=-1)
        my_slope = lax.dynamic_slice_in_dim(slope, me * tok_rows, tok_rows, 1)
        common = (my_slope * shared[None, :]).astype(jnp.bfloat16)
        grads[t] = (normed, hidden_w, grad_all, grad_acts, route, common, own(normed))
        if u + 1 < ticks:
            partial = dot_plain(
                jnp.concatenate([grad_acts, route], axis=1), both_w.T
            ).astype(jnp.bfloat16)
            grad_normed = jnp.sum(give_back(sizes, partial, 1).astype(jnp.float32), axis=0)
            grad_normed = grad_normed - contract_first(common, router_t)
            hidden_f = layer_in.astype(jnp.float32)
            inv_rms = lax.rsqrt(jnp.mean(hidden_f * hidden_f, axis=-1, keepdims=True) + norm_eps)
            normed_f = hidden_f * inv_rms
            grad_in = (
                grad_f
                + inv_rms
                * (grad_normed - normed_f * jnp.mean(grad_normed * normed_f, axis=-1, keepdims=True))
            ).astype(jnp.bfloat16)

    def totals(begin):
        chosen_ticks = grads[begin : begin + micro_count]
        normed, hidden_w, grad_all, grad_acts, route, common, normed_own = [
            jnp.concatenate(parts, axis=1 if n == 5 else 0)
            for n, parts in enumerate(zip(*chosen_ticks))
        ]
        first = contract_first(route, normed)[:expert_count]
        return (
            first - dot_plain(common, normed_own),
            contract_first(normed, grad_acts[:, :hidden_dim]).astype(jnp.bfloat16),
            contract_first(normed, grad_acts[:, hidden_dim:]).astype(jnp.bfloat16),
            contract_first(hidden_w, grad_all).astype(jnp.bfloat16),
        )

    router_sum, grad_gate, grad_up, grad_down = lax.switch(
        s, [functools.partial(totals, begin) for begin in range(sections)])
    router_out = lax.psum(router_sum, group).T[None]
    mean_loss = loss_total / (micro_count * tok_rows * experts * cores)
    return (
        mean_loss,
        head_total,
        router_out,
        grad_gate[None, None],
        grad_up[None, None],
        grad_down[None, None],
    )


def solution(mesh):
    sizes = tuple(mesh.shape[axis] for axis in ("section", "expert", "dp"))
    return jax.shard_map(
        functools.partial(shards, sizes),
        mesh=mesh,
        in_specs=(
            P(None, ("expert", "dp"), None),
            P("section", None, ("expert", "dp"), None),
            P(None, ("expert", "dp")),
            P("section", None, None),
            P(),
            P("section", ("expert", "dp"), None, None),
            P("section", ("expert", "dp"), None, None),
            P("section", ("expert", "dp"), None, None),
        ),
        out_specs=(
            P(),
            P(),
            P("section", None, None),
            P("section", ("expert", "dp"), None, None),
            P("section", ("expert", "dp"), None, None),
            P("section", ("expert", "dp"), None, None),
        ),
        check_vma=False,
    )
```

time: 1850 us -> 952 us (0.51); the launches traced: 1820 us -> 944 us
  local copies, waits for them, and re-layouts: 799 us -> 26.8 us
  Pallas kernels: 0 us -> 476 us
  waiting for transfers between devices: 373 us -> 144 us
  matrix products: 290 us -> 137 us
  starting transfers between devices: 127 us -> 0.08 us
  blocking collectives: 95.2 us -> 48.3 us
  other arithmetic: 120 us -> 81.3 us
    scatter x20 -> x0, local copies, waits for them, and re-layouts: 496 us -> none  [the longest x10 433 us: shards(): outgoing = jnp.zeros((expert_count, slot_count, model_width), jnp.bfloat1...]
    pallas_call x0 -> x19, Pallas kernels: none -> 476 us  [the longest x9 260 us: give_back(): pl.pallas_call(functools.partial(give_back_kernel, sizes), out_shape=jax....]
    all_to_all x23 -> x0, waiting for transfers between devices: 311 us -> none  [the longest x14 210 us: route_rows(): lax.all_to_all(payload, ('expert', 'dp'), split_axis=0, concat_axis=0, ti...]
    gather x18 -> x0, local copies, waits for them, and re-layouts: 158 us -> none  [the longest x9 94.2 us: shards(): returned[jnp.minimum(target, expert_count - 1), slot_of]]
    psum x2, waiting for transfers between devices: 29.6 us -> 144 us  [the longest x1 136 us: shards(): lax.psum((head_term, loss_term), ('section',) + group)]
    all_to_all x23 -> x0, starting transfers between devices: 101 us -> none  [the longest x14 63.1 us: route_rows(): lax.all_to_all(payload, ('expert', 'dp'), split_axis=0, concat_axis=0, ti...]
    dot_general x21 -> x9, matrix products: 111 us -> 23 us  [contract_first(): lax.dot_general(left, right, (((0,), (0,)), ((), ())), preferred_element_...]
    dot_general x31 -> x16, matrix products: 128 us -> 73 us  [dot_plain(): return jnp.dot(left, right, preferred_element_type=jnp.float32)]
  transfers between devices with their start and end apart: 33 -> 2, of which waited for: 25 -> 2; matrix products, arithmetic and copies ran while one was open for 34% -> 0% of each run, Pallas kernels for 0% -> 0%
where the time goes in v1:
time: 952 us; the launch traced here: 944 us
  Pallas kernels  476 us (50%)
  waiting for transfers between devices  144 us (15%)
  matrix products  137 us (14%)
  other arithmetic  81.3 us (9%)
  blocking collectives  48.3 us (5%)
  local copies, waits for them, and re-layouts  26.8 us (3%)
  between operations  18.3 us (2%)
  loops' own time  12.6 us (1%)
    pallas_call x9, Pallas kernels, give_back(): pl.pallas_call(functools.partial(give_back_kernel, sizes), out_shape=jax....  260 us
    pallas_call x10, Pallas kernels, relay(): pl.pallas_call(functools.partial(relay_kernel, sizes, chunks, step, first...  216 us
    psum x1, waiting for transfers between devices, shards(): lax.psum((head_term, loss_term), ('section',) + group)  136 us
    dot_general x16, matrix products, dot_plain(): return jnp.dot(left, right, preferred_element_type=jnp.float32)  73 us
    dot_general x11, matrix products, contract_last(): lax.dot_general(left, right, (((1,), (1,)), ((), ())), preferred_element_...  40.6 us
    psum x1, blocking collectives, shards(): lax.psum((head_term, loss_term), ('section',) + group)  37.8 us
    dot_general x9, matrix products, contract_first(): lax.dot_general(left, right, (((0,), (0,)), ((), ())), preferred_element_...  23 us
    reduce_sum x9, other arithmetic, shards(): jnp.mean(hidden_f * hidden_f, axis=-1, keepdims=True) + norm_eps  20 us
  transfers between devices with their start and end apart: 2, of which 2 were waited for; matrix products, arithmetic and copies ran while one was open for 0% of the time, Pallas kernels for 0%

profile of v1, /device:TPU:0, one launch (start us, length us, event | category | flops | bytes accessed | tf_op | source)
XLA Modules:
  0.0 944.4 jit_solution(16344846245566626604)
XLA Ops:
  10.0 20.8 %shard_map.127 = bf16[8,64,2048]{2,1,0:T(8,128)(2,1)} custom-call(bf16[64,2048]{1,0:T(8,128)(2,1)} %broadcast_21_carried_ref.2.carried_ref, bf16[64,2048]{1,0:T(8,128)(2,1)} %get-tuple-element.279.root_ref), custom_call_target="tpu_custom_call" | custom-call | tf_op jit(solution)/shard_map/pallas_call | solution.py:135
  35.0 10.5 %all-gather = s32[1,2,512,4]{3,1,0,2:T(2,128)} all-gather(s32[1,2,64,4]{3,1,0,2:T(2,128)S(1)} %copy.19), channel_id=2, replica_groups=mesh['section'=4,'expert'=4,'dp'=2] {'expert','dp'}, dimensions={2}, use_global_device_ids=true | all-gather | bytes 18432 | tf_op jit(solution)/shard_map/all_gather | solution.py:212
  62.2 28.9 %shard_map.128 = bf16[8,64,2048]{2,1,0:T(8,128)(2,1)} custom-call(bf16[8,64,2048]{2,1,0:T(8,128)(2,1)} %bitcast.313), custom_call_target="tpu_custom_call" | custom-call | tf_op jit(solution)/shard_map/pallas_call | solution.py:186
  95.8 20.9 %shard_map.129 = bf16[8,64,2048]{2,1,0:T(8,128)(2,1)} custom-call(bf16[64,2048]{1,0:T(8,128)(2,1)} %add_convert_fusion.carried_ref, bf16[64,2048]{1,0:T(8,128)(2,1)} %get-tuple-element.278.root_ref), custom_call_target="tpu_custom_call" | custom-call | tf_op jit(solution)/shard_map/pallas_call | solution.py:135
  134.6 28.2 %shard_map.130 = bf16[8,64,2048]{2,1,0:T(8,128)(2,1)} custom-call(bf16[8,64,2048]{2,1,0:T(8,128)(2,1)} %bitcast.314), custom_call_target="tpu_custom_call" | custom-call | tf_op jit(solution)/shard_map/pallas_call | solution.py:186
  168.0 21.4 %shard_map.131 = bf16[8,64,2048]{2,1,0:T(8,128)(2,1)} custom-call(bf16[64,2048]{1,0:T(8,128)(2,1)} %get-tuple-element.264.carried_ref, bf16[64,2048]{1,0:T(8,128)(2,1)} %get-tuple-element.278.root_ref), custom_call_target="tpu_custom_call" | custom-call | tf_op jit(solution)/shard_map/pallas_call | solution.py:135
  206.4 28.9 %shard_map.132 = bf16[8,64,2048]{2,1,0:T(8,128)(2,1)} custom-call(bf16[8,64,2048]{2,1,0:T(8,128)(2,1)} %bitcast.315), custom_call_target="tpu_custom_call" | custom-call | tf_op jit(solution)/shard_map/pallas_call | solution.py:186
  240.5 21.2 %shard_map.133 = bf16[8,64,2048]{2,1,0:T(8,128)(2,1)} custom-call(bf16[64,2048]{1,0:T(8,128)(2,1)} %get-tuple-element.266.carried_ref, bf16[64,2048]{1,0:T(8,128)(2,1)} %get-tuple-element.278.root_ref), custom_call_target="tpu_custom_call" | custom-call | tf_op jit(solution)/shard_map/pallas_call | solution.py:135
  278.8 28.3 %shard_map.134 = bf16[8,64,2048]{2,1,0:T(8,128)(2,1)} custom-call(bf16[8,64,2048]{2,1,0:T(8,128)(2,1)} %bitcast.316), custom_call_target="tpu_custom_call" | custom-call | tf_op jit(solution)/shard_map/pallas_call | solution.py:186
  312.3 21.7 %shard_map.135 = bf16[8,64,2048]{2,1,0:T(8,128)(2,1)} custom-call(bf16[64,2048]{1,0:T(8,128)(2,1)} %get-tuple-element.268.carried_ref, bf16[64,2048]{1,0:T(8,128)(2,1)} %get-tuple-element.278.root_ref), custom_call_target="tpu_custom_call" | custom-call | tf_op jit(solution)/shard_map/pallas_call | solution.py:135
  351.0 28.7 %shard_map.136 = bf16[8,64,2048]{2,1,0:T(8,128)(2,1)} custom-call(bf16[8,64,2048]{2,1,0:T(8,128)(2,1)} %bitcast.317), custom_call_target="tpu_custom_call" | custom-call | tf_op jit(solution)/shard_map/pallas_call | solution.py:186
  390.0 23.7 %shard_map.137 = bf16[8,64,2048]{2,1,0:T(8,128)(2,1)} custom-call(bf16[64,2048]{1,0:T(8,128)(2,1)} %broadcast_21_carried_ref.2.carried_ref, bf16[64,2048]{1,0:T(8,128)(2,1)} %get-tuple-element.277.root_ref), custom_call_target="tpu_custom_call" | custom-call | tf_op jit(solution)/shard_map/pallas_call | solution.py:135
  430.3 29.5 %shard_map.138 = bf16[8,64,2048]{2,1,0:T(8,128)(2,1)} custom-call(bf16[8,64,2048]{2,1,0:T(8,128)(2,1)} %bitcast.318), custom_call_target="tpu_custom_call" | custom-call | tf_op jit(solution)/shard_map/pallas_call | solution.py:186
  465.2 22.1 %shard_map.139 = bf16[8,64,2048]{2,1,0:T(8,128)(2,1)} custom-call(bf16[64,2048]{1,0:T(8,128)(2,1)} %fusion.206.carried_ref, bf16[64,2048]{1,0:T(8,128)(2,1)} %get-tuple-element.276.root_ref), custom_call_target="tpu_custom_call" | custom-call | tf_op jit(solution)/shard_map/pallas_call | solution.py:135
  504.7 29.4 %shard_map.140 = bf16[8,64,2048]{2,1,0:T(8,128)(2,1)} custom-call(bf16[8,64,2048]{2,1,0:T(8,128)(2,1)} %bitcast.311), custom_call_target="tpu_custom_call" | custom-call | tf_op jit(solution)/shard_map/pallas_call | solution.py:186
  539.6 22.2 %shard_map.141 = bf16[8,64,2048]{2,1,0:T(8,128)(2,1)} custom-call(bf16[64,2048]{1,0:T(8,128)(2,1)} %fusion.208.carried_ref, bf16[64,2048]{1,0:T(8,128)(2,1)} %get-tuple-element.276.root_ref), custom_call_target="tpu_custom_call" | custom-call | tf_op jit(solution)/shard_map/pallas_call | solution.py:135
  575.3 29.5 %shard_map.142 = bf16[8,64,2048]{2,1,0:T(8,128)(2,1)} custom-call(bf16[8,64,2048]{2,1,0:T(8,128)(2,1)} %bitcast.312), custom_call_target="tpu_custom_call" | custom-call | tf_op jit(solution)/shard_map/pallas_call | solution.py:186
  610.2 20.9 %shard_map.143 = bf16[8,64,2048]{2,1,0:T(8,128)(2,1)} custom-call(bf16[64,2048]{1,0:T(8,128)(2,1)} %fusion.210.carried_ref, bf16[64,2048]{1,0:T(8,128)(2,1)} %get-tuple-element.276.root_ref), custom_call_target="tpu_custom_call" | custom-call | tf_op jit(solution)/shard_map/pallas_call | solution.py:135
  646.3 28.4 %shard_map.144 = bf16[8,64,2048]{2,1,0:T(8,128)(2,1)} custom-call(bf16[8,64,2048]{2,1,0:T(8,128)(2,1)} %bitcast.310), custom_call_target="tpu_custom_call" | custom-call | tf_op jit(solution)/shard_map/pallas_call | solution.py:186
  680.8 21.3 %shard_map.145 = bf16[8,64,2048]{2,1,0:T(8,128)(2,1)} custom-call(bf16[64,2048]{1,0:T(8,128)(2,1)} %fusion.212.carried_ref, bf16[64,2048]{1,0:T(8,128)(2,1)} %get-tuple-element.276.root_ref), custom_call_target="tpu_custom_call" | custom-call | tf_op jit(solution)/shard_map/pallas_call | solution.py:135
  712.2 33.0 %conditional.1 = (f32[8,2048]{1,0:T(8,128)S(1)}, bf16[1,1,2048,768]{3,2,1,0:T(8,128)(2,1)}, bf16[1,1,2048,768]{3,2,1,0:T(8,128)(2,1)}, bf16[1,1,768,2048]{3,2,1,0:T(8,128)(2,1)}) conditional(s32[]{:T(128)} %clamp.3, (bf16[512,128]{1,0:T(8,128)(2,1)S(1)}, bf16[512,128]{1,0:T(8,128)(2,1)}, bf16[512,2048]{1,0:T(8,128)(2,1)}, ...), branch_computations={%region_43.44_spmd, %region_44.45_spmd, %region_45.46_spmd, %regio... | conditional | flops 9718779904 | bytes 92735784 | solution.py:318
  749.6 37.8 %psum.21 = f32[]{:T(128)} all-reduce(f32[]{:T(128)S(6)} %select_n.71), channel_id=1, replica_groups=mesh['section'=4,'expert'=4,'dp'=2] {'section','expert','dp'}, use_global_device_ids=true, to_apply=%region_19.20 | all-reduce | flops 1 | bytes 8 | tf_op jit(solution)/shard_map/psum | solution.py:266
  788.1 8.4 all-reduce.6.cloned.1.call-done
  796.6 135.8 %all-reduce.4.cloned.1.call-done = f32[2048,128]{1,0:T(8,128)} async-done(((f32[2048,128]{1,0:T(8,128)}), f32[2048,128]{1,0:T(8,128)}) %all-reduce.4.cloned.1.call-update) | async-done | bytes 1048592 | tf_op jit(solution)/shard_map/psum | solution.py:266
  (340 shorter events, 244.8 us)
Async XLA Ops:
  7.2 51.9 %copy-start = (bf16[1,1,768,2048]{3,2,1,0:T(8,128)(2,1)S(1)}, bf16[1,1,768,2048]{3,2,1,0:T(8,128)(2,1)}, u32[]{:S(2)}) copy-start(bf16[1,1,768,2048]{3,2,1,0:T(8,128)(2,1)} %param.19) | copy-start | bytes 9437188
  7.2 789.4 %all-reduce.6.cloned.1.call-start = ((), (), s32[]{:S(2)}) async-start(), calls=%async_computation.1 | async-start | bytes 131072 | tf_op jit(solution)/shard_map/psum | solution.py:320
  34.8 15.5 %copy-start.33 = (bf16[1,2048,8]{1,2,0:T(8,128)(2,1)S(1)}, bf16[1,2048,8]{1,2,0:T(8,128)(2,1)}, u32[]{:S(2)}) copy-start(bf16[1,2048,8]{1,2,0:T(8,128)(2,1)} %param.15) | copy-start | bytes 98308
  351.0 34.6 %copy-start.50 = (bf16[64,2048]{1,0:T(8,128)(2,1)S(1)}, bf16[64,2048]{1,0:T(8,128)(2,1)}, u32[]{:S(2)}) copy-start(bf16[64,2048]{1,0:T(8,128)(2,1)} %get-tuple-element.268.carried_ref) | copy-start | bytes 786436
  387.7 27.3 %copy-start.96 = (f32[1,512]{1,0:T(1,128)S(1)}, f32[1,512]{1,0:T(1,128)}, u32[]{:S(2)}) copy-start(f32[1,512]{1,0:T(1,128)} %copy-done.95) | copy-start | bytes 6148
  421.4 74.6 %copy-start.85 = (pred[128]{0:T(512)(128)(4,1)}, pred[128]{0:T(512)(128)(4,1)S(1)}, u32[]{:S(2)}) copy-start(pred[128]{0:T(512)(128)(4,1)S(1)} %iota_compare_fusion.3) | copy-start | bytes 388
  422.6 7.7 copy-start.66
  430.3 31.5 %copy-start.106 = (f32[64]{0:T(128)S(1)}, f32[64]{0:T(128)}, u32[]{:S(2)}) copy-start(f32[64]{0:T(128)} %get-tuple-element.269) | copy-start | bytes 772
  461.8 25.6 %copy-start.94 = (f32[1,512]{1,0:T(1,128)S(1)}, f32[1,512]{1,0:T(1,128)}, u32[]{:S(2)}) copy-start(f32[1,512]{1,0:T(1,128)} %copy-done.93) | copy-start | bytes 6148
  461.9 30.8 %copy-start.97 = (bf16[8,64]{1,0:T(8,128)(2,1)}, bf16[8,64]{1,0:T(8,128)(2,1)S(1)}, u32[]{:S(2)}) copy-start(bf16[8,64]{1,0:T(8,128)(2,1)S(1)} %fusion.238) | copy-start | bytes 3076
  487.4 8.8 copy-start.64
  487.4 8.8 copy-start.65
  504.7 31.5 %copy-start.105 = (f32[64]{0:T(128)S(1)}, f32[64]{0:T(128)}, u32[]{:S(2)}) copy-start(f32[64]{0:T(128)} %get-tuple-element.267) | copy-start | bytes 772
  536.2 25.6 %copy-start.92 = (f32[1,512]{1,0:T(1,128)S(1)}, f32[1,512]{1,0:T(1,128)}, u32[]{:S(2)}) copy-start(f32[1,512]{1,0:T(1,128)} %copy-done.91) | copy-start | bytes 6148
  561.8 8.2 copy-start.115
  575.3 31.5 %copy-start.104 = (f32[64]{0:T(128)S(1)}, f32[64]{0:T(128)}, u32[]{:S(2)}) copy-start(f32[64]{0:T(128)} %get-tuple-element.265) | copy-start | bytes 772
  606.8 24.3 %copy-start.90 = (f32[1,512]{1,0:T(1,128)S(1)}, f32[1,512]{1,0:T(1,128)}, u32[]{:S(2)}) copy-start(f32[1,512]{1,0:T(1,128)} %copy-done.89) | copy-start | bytes 6148
  631.1 9.9 %copy-start.116 = (bf16[1,1,2048,768]{3,2,1,0:T(8,128)(2,1)S(1)}, bf16[1,1,2048,768]{3,2,1,0:T(8,128)(2,1)}, u32[]{:S(2)}) copy-start(bf16[1,1,2048,768]{3,2,1,0:T(8,128)(2,1)} %param.17) | copy-start | bytes 9437188
  646.3 30.5 %copy-start.103 = (f32[64]{0:T(128)S(1)}, f32[64]{0:T(128)}, u32[]{:S(2)}) copy-start(f32[64]{0:T(128)} %get-tuple-element.263) | copy-start | bytes 772
  676.7 25.4 %copy-start.88 = (f32[1,512]{1,0:T(1,128)S(1)}, f32[1,512]{1,0:T(1,128)}, u32[]{:S(2)}) copy-start(f32[1,512]{1,0:T(1,128)} %copy-done.87) | copy-start | bytes 6148
  712.2 33.7 %copy-start.101 = (f32[128]{0:T(128)S(1)}, f32[128]{0:T(128)}, u32[]{:S(2)}) copy-start(f32[128]{0:T(128)} %copy-done.100) | copy-start | bytes 1540
  712.2 33.7 %copy-start.102 = (s32[128]{0:T(128)S(1)}, s32[128]{0:T(128)}, u32[]{:S(2)}) copy-start(s32[128]{0:T(128)} %eq.54) | copy-start | bytes 1540
  712.2 36.1 %copy-start.117 = (f32[128]{0:T(128)S(1)}, f32[128]{0:T(128)}, u32[]{:S(2)}) copy-start(f32[128]{0:T(128)} %get-tuple-element.252) | copy-start | bytes 1540
  745.9 186.5 %all-reduce.4.cloned.1.call-start = ((), (), s32[]{:S(2)}) async-start(), calls=%async_computation | async-start | bytes 2097152 | tf_op jit(solution)/shard_map/psum | solution.py:266
  (69 other events, 253.6 us)
Sparse Core Ops, SparseCore 0:
  746.0 50.4 all-reduce.5
  802.3 130.0 all-reduce.3

commit v2 on v1

--- a/solution.py
+++ b/solution.py
@@ -143,52 +143,76 @@
             dma((chunks, cores - 1)), dma((chunks, cores - 1)),
             dma((chunks, cores - 1, experts - 1)), dma((chunks, cores - 1, experts - 1)),
         ],
+        cost_estimate=pl.CostEstimate(
+            flops=0, bytes_accessed=30 * experts * cores * carried.size * 2, transcendentals=0),
         compiler_params=pltpu.CompilerParams(collective_id=call_id, has_side_effects=True),
     )(carried, root)
     return out.reshape(experts * cores * rows, width)
 
 
-def give_back_kernel(sizes, parts_ref, out_ref, own_sem, send_sem, recv_sem):
+def give_back_kernel(sizes, parts_ref, out_ref, stage_ref, sum_ref, d_send, d_recv, x_send, x_recv):
     sections, experts, cores = sizes
     e, d = lax.axis_index("expert"), lax.axis_index("dp")
-    me = e * cores + d
-    peers = [(x, c) for x in range(experts) for c in range(cores) if (x, c) != (0, 0)]
-
-    def place(x, c):
-        return lax.rem(e + x, experts), lax.rem(d + c, cores)
 
     barrier = pltpu.get_barrier_semaphore()
-    for x, c in peers:
-        to_e, to_d = place(x, c)
-        pl.semaphore_signal(barrier, inc=1, device_id={"expert": to_e, "dp": to_d}, device_id_type=MESH)
-    pl.semaphore_wait(barrier, len(peers))
-    own = pltpu.make_async_copy(parts_ref.at[me], out_ref.at[me], own_sem)
-    copies = []
-    for n, (x, c) in enumerate(peers):
-        to_e, to_d = place(x, c)
-        copies.append(pltpu.make_async_remote_copy(
-            src_ref=parts_ref.at[to_e * cores + to_d], dst_ref=out_ref.at[me],
-            send_sem=send_sem.at[n], recv_sem=recv_sem.at[n],
-            device_id={"expert": to_e, "dp": to_d}, device_id_type=MESH))
-    for copy in copies:
-        copy.start()
-    own.start()
-    own.wait()
-    for copy in copies:
-        copy.wait()
+    for off in range(1, experts):
+        pl.semaphore_signal(barrier, inc=1, device_id={"expert": lax.rem(e + off, experts)}, device_id_type=MESH)
+    for off in range(1, cores):
+        pl.semaphore_signal(barrier, inc=1, device_id={"dp": lax.rem(d + off, cores)}, device_id_type=MESH)
+    pl.semaphore_wait(barrier, experts + cores - 2)
+
+    def beside(off, core_off):
+        to_d = lax.rem(d + core_off, cores)
+        return pltpu.make_async_remote_copy(
+            src_ref=parts_ref.at[lax.rem(e + off, experts) * cores + to_d],
+            dst_ref=stage_ref.at[core_off - 1, off],
+            send_sem=d_send.at[core_off - 1, off], recv_sem=d_recv.at[core_off - 1, off],
+            device_id={"dp": to_d}, device_id_type=MESH)
+
+    def across(off):
+        return pltpu.make_async_remote_copy(
+            src_ref=sum_ref.at[off - 1], dst_ref=out_ref.at[e],
+            send_sem=x_send.at[off - 1], recv_sem=x_recv.at[off - 1],
+            device_id={"expert": lax.rem(e + off, experts)}, device_id_type=MESH)
+
+    order = [off for off in range(experts - 1, 0, -1)] + [0]
+    for off in order:
+        for core_off in range(1, cores):
+            beside(off, core_off).start()
+    for n, off in enumerate(order):
+        total = parts_ref[lax.rem(e + off, experts) * cores + d].astype(jnp.float32)
+        for core_off in range(1, cores):
+            beside(off, core_off).wait_recv()
+            total = total + stage_ref[core_off - 1, off].astype(jnp.float32)
+        if off == 0:
+            out_ref[e] = total.astype(out_ref.dtype)
+        else:
+            sum_ref[off - 1] = total.astype(out_ref.dtype)
+        if n > 0:
+            across(order[n - 1]).start()
+    for off in range(1, experts):
+        across(off).wait()
+    for off in order:
+        for core_off in range(1, cores):
+            beside(off, core_off).wait_send()
 
 
 def give_back(sizes, parts, call_id):
     sections, experts, cores = sizes
-    count = experts * cores
+    block = parts.shape[1:]
     dma = pltpu.SemaphoreType.DMA
-    parts = parts.reshape(count, parts.shape[0] // count, parts.shape[1])
     return pl.pallas_call(
         functools.partial(give_back_kernel, sizes),
-        out_shape=jax.ShapeDtypeStruct(parts.shape, parts.dtype),
+        out_shape=jax.ShapeDtypeStruct((experts,) + block, parts.dtype),
         in_specs=[pl.BlockSpec(memory_space=pltpu.VMEM)],
         out_specs=pl.BlockSpec(memory_space=pltpu.VMEM),
-        scratch_shapes=[dma(()), dma((count - 1,)), dma((count - 1,))],
+        scratch_shapes=[
+            pltpu.VMEM((cores - 1, experts) + block, parts.dtype),
+            pltpu.VMEM((experts - 1,) + block, parts.dtype),
+            dma((cores - 1, experts)), dma((cores - 1, experts)),
+            dma((experts - 1,)), dma((experts - 1,)),
+        ],
+        cost_estimate=pl.CostEstimate(flops=0, bytes_accessed=30 * parts.size * 2, transcendentals=0),
         compiler_params=pltpu.CompilerParams(collective_id=call_id, has_side_effects=True),
     )(parts)
 
@@ -216,6 +240,9 @@
 
     def own(rows_all):
         return lax.dynamic_slice_in_dim(rows_all, me * tok_rows, tok_rows, 0)
+
+    def by_device(rows_all):
+        return rows_all.reshape(experts * cores, tok_rows, width)
 
     kept = []
     finals = []
@@ -240,7 +267,7 @@
         d_gate = (mine * up_act * sig * (1.0 + gate_act * (1.0 - sig))).astype(jnp.bfloat16)
         d_up = (mine * silu).astype(jnp.bfloat16)
         partial = dot_plain(hidden_w, down_w).astype(jnp.bfloat16)
-        mix = jnp.sum(give_back(sizes, partial, 1).astype(jnp.float32), axis=0)
+        mix = jnp.sum(give_back(sizes, by_device(partial), 1).astype(jnp.float32), axis=0)
         layer_in = own(hidden_all)
         layer_out = (layer_in.astype(jnp.float32) + mix).astype(jnp.bfloat16)
         kept.append((layer_in, mix, normed, chosen, slope, hidden_w, d_gate, d_up))
@@ -263,7 +290,9 @@
     loss_term = jnp.where(is_last, jnp.sum(token_loss), 0.0)
     grad_top = contract_last(grad_logits, class_head).astype(jnp.bfloat16)
     grad_top = grad_top.reshape(micro_count, tok_rows, width)
-    head_total, loss_total = lax.psum((head_term, loss_term), ("section",) + group)
+    loss_row = jnp.full((8, head_term.shape[1]), loss_term, jnp.float32)
+    summed = lax.psum(jnp.concatenate([head_term, loss_row], axis=0), ("section",) + group)
+    head_total, loss_total = summed[:width], summed[width, 0]
 
     grads = [None] * ticks
     grad_in = jnp.zeros((tok_rows, width), jnp.bfloat16)
@@ -290,7 +319,7 @@
             partial = dot_plain(
                 jnp.concatenate([grad_acts, route], axis=1), both_w.T
             ).astype(jnp.bfloat16)
-            grad_normed = jnp.sum(give_back(sizes, partial, 1).astype(jnp.float32), axis=0)
+            grad_normed = jnp.sum(give_back(sizes, by_device(partial), 1).astype(jnp.float32), axis=0)
             grad_normed = grad_normed - contract_first(common, router_t)
             hidden_f = layer_in.astype(jnp.float32)
             inv_rms = lax.rsqrt(jnp.mean(hidden_f * hidden_f, axis=-1, keepdims=True) + norm_eps)
@@ -317,7 +346,8 @@
 
     router_sum, grad_gate, grad_up, grad_down = lax.switch(
         s, [functools.partial(totals, begin) for begin in range(sections)])
-    router_out = lax.psum(router_sum, group).T[None]
+    copies = jnp.broadcast_to(router_sum[None], (experts * cores,) + router_sum.shape)
+    router_out = jnp.sum(give_back(sizes, copies, 3), axis=0).T[None]
     mean_loss = loss_total / (micro_count * tok_rows * experts * cores)
     return (
         mean_loss,

time: 952 us -> 694 us (0.73)
  waiting for transfers between devices: 144 us -> 0.02 us
  Pallas kernels: 476 us -> 400 us
  blocking collectives: 48.3 us -> 10.5 us
    psum x2 -> x1, waiting for transfers between devices: 144 us -> 0.01 us  [shards(): lax.psum(jnp.concatenate([head_term, loss_row], axis=0), ('section',) + g...]
    pallas_call x9 -> x10, Pallas kernels: 260 us -> 192 us  [give_back(): pl.pallas_call(functools.partial(give_back_kernel, sizes), out_shape=jax....]
    psum x1 -> x0, blocking collectives: 37.8 us -> none  [shards(): lax.psum((head_term, loss_term), ('section',) + group)]
    reduce_sum x9 -> x10, other arithmetic: 19.7 us -> 16.2 us  [the longest x9 14.6 us: shards(): jnp.sum(give_back(sizes, by_device(partial), 1).astype(jnp.float32), axis=0)]
  transfers between devices with their start and end apart: 2 -> 1, of which waited for: 2 -> 0; matrix products, arithmetic and copies ran while one was open for 0% -> 17% of each run, Pallas kernels for 0% -> 29%
where the time goes in v2:
time: 694 us; the launch traced here: 686 us
  Pallas kernels  400 us (58%)
  matrix products  136 us (20%)
  other arithmetic  79.8 us (11%)
  local copies, waits for them, and re-layouts  28.9 us (4%)
  between operations  18.2 us (3%)
  loops' own time  12.1 us (2%)
  blocking collectives  10.5 us (2%)
    pallas_call x10, Pallas kernels, relay(): pl.pallas_call(functools.partial(relay_kernel, sizes, chunks, step, first...  209 us
    pallas_call x10, Pallas kernels, give_back(): pl.pallas_call(functools.partial(give_back_kernel, sizes), out_shape=jax....  192 us
    dot_general x16, matrix products, dot_plain(): return jnp.dot(left, right, preferred_element_type=jnp.float32)  72.3 us
    dot_general x11, matrix products, contract_last(): lax.dot_general(left, right, (((1,), (1,)), ((), ())), preferred_element_...  40.6 us
    dot_general x9, matrix products, contract_first(): lax.dot_general(left, right, (((0,), (0,)), ((), ())), preferred_element_...  22.6 us
    reduce_sum x9, other arithmetic, shards(): jnp.mean(hidden_f * hidden_f, axis=-1, keepdims=True) + norm_eps  20.1 us
    reduce_sum x9, other arithmetic, shards(): jnp.sum(give_back(sizes, by_device(partial), 1).astype(jnp.float32), axis=0)  14.6 us
    convert_element_type x10, other arithmetic, shards(): normed = (hidden_f * inv_rms).astype(jnp.bfloat16)  14 us
  transfers between devices with their start and end apart: 1, of which 0 were waited for; matrix products, arithmetic and copies ran while one was open for 17% of the time, Pallas kernels for 29%

profile of v2, /device:TPU:0, one launch (start us, length us, event | category | flops | bytes accessed | tf_op | source)
XLA Modules:
  0.0 685.6 jit_solution(10256417048822841248)
XLA Ops:
  10.0 20.8 %shard_map.127 = bf16[8,64,2048]{2,1,0:T(8,128)(2,1)} custom-call(bf16[64,2048]{1,0:T(8,128)(2,1)} %broadcast_21_carried_ref.2.carried_ref, bf16[64,2048]{1,0:T(8,128)(2,1)} %get-tuple-element.279.root_ref), custom_call_target="tpu_custom_call" | custom-call | bytes 62914560 | tf_op jit(solution)/shard_map/pallas_call | solution.py:135
  35.0 10.5 %all-gather = s32[1,2,512,4]{3,1,0,2:T(2,128)} all-gather(s32[1,2,64,4]{3,1,0,2:T(2,128)S(1)} %copy.19), channel_id=2, replica_groups=mesh['section'=4,'expert'=4,'dp'=2] {'expert','dp'}, dimensions={2}, use_global_device_ids=true | all-gather | bytes 18432 | tf_op jit(solution)/shard_map/all_gather | solution.py:236
  51.6 6.9 %fusion.276 = f32[512,1536]{1,0:T(8,128)S(1)} fusion(bf16[512,2048]{1,0:T(8,128)(2,1)} %multiply_convert_fusion.4, bf16[2048,768]{1,0:T(8,128)(2,1)} %bitcast.341, bf16[2048,768]{1,0:T(8,128)(2,1)} %bitcast.350), kind=kOutput, calls=%fused_computation.459 | convolution fusion | flops 3233808384 | bytes 11534336 | tf_op jit(solution)/shard_map/dot_general | solution.py:22
  62.2 19.9 %shard_map.128 = bf16[4,64,2048]{2,1,0:T(8,128)(2,1)} custom-call(bf16[8,64,2048]{2,1,0:T(8,128)(2,1)} %bitcast.314), custom_call_target="tpu_custom_call" | custom-call | bytes 62914560 | tf_op jit(solution)/shard_map/pallas_call | solution.py:204
  86.2 20.9 %shard_map.129 = bf16[8,64,2048]{2,1,0:T(8,128)(2,1)} custom-call(bf16[64,2048]{1,0:T(8,128)(2,1)} %add_convert_fusion.carried_ref, bf16[64,2048]{1,0:T(8,128)(2,1)} %get-tuple-element.278.root_ref), custom_call_target="tpu_custom_call" | custom-call | bytes 62914560 | tf_op jit(solution)/shard_map/pallas_call | solution.py:135
  125.0 20.0 %shard_map.130 = bf16[4,64,2048]{2,1,0:T(8,128)(2,1)} custom-call(bf16[8,64,2048]{2,1,0:T(8,128)(2,1)} %bitcast.315), custom_call_target="tpu_custom_call" | custom-call | bytes 62914560 | tf_op jit(solution)/shard_map/pallas_call | solution.py:204
  149.5 19.3 %shard_map.131 = bf16[8,64,2048]{2,1,0:T(8,128)(2,1)} custom-call(bf16[64,2048]{1,0:T(8,128)(2,1)} %get-tuple-element.264.carried_ref, bf16[64,2048]{1,0:T(8,128)(2,1)} %get-tuple-element.278.root_ref), custom_call_target="tpu_custom_call" | custom-call | bytes 62914560 | tf_op jit(solution)/shard_map/pallas_call | solution.py:135
  185.8 20.1 %shard_map.132 = bf16[4,64,2048]{2,1,0:T(8,128)(2,1)} custom-call(bf16[8,64,2048]{2,1,0:T(8,128)(2,1)} %bitcast.316), custom_call_target="tpu_custom_call" | custom-call | bytes 62914560 | tf_op jit(solution)/shard_map/pallas_call | solution.py:204
  210.5 20.4 %shard_map.133 = bf16[8,64,2048]{2,1,0:T(8,128)(2,1)} custom-call(bf16[64,2048]{1,0:T(8,128)(2,1)} %get-tuple-element.266.carried_ref, bf16[64,2048]{1,0:T(8,128)(2,1)} %get-tuple-element.278.root_ref), custom_call_target="tpu_custom_call" | custom-call | bytes 62914560 | tf_op jit(solution)/shard_map/pallas_call | solution.py:135
  247.9 20.0 %shard_map.134 = bf16[4,64,2048]{2,1,0:T(8,128)(2,1)} custom-call(bf16[8,64,2048]{2,1,0:T(8,128)(2,1)} %bitcast.317), custom_call_target="tpu_custom_call" | custom-call | bytes 62914560 | tf_op jit(solution)/shard_map/pallas_call | solution.py:204
  272.5 19.7 %shard_map.135 = bf16[8,64,2048]{2,1,0:T(8,128)(2,1)} custom-call(bf16[64,2048]{1,0:T(8,128)(2,1)} %get-tuple-element.268.carried_ref, bf16[64,2048]{1,0:T(8,128)(2,1)} %get-tuple-element.278.root_ref), custom_call_target="tpu_custom_call" | custom-call | bytes 62914560 | tf_op jit(solution)/shard_map/pallas_call | solution.py:135
  309.2 20.1 %shard_map.136 = bf16[4,64,2048]{2,1,0:T(8,128)(2,1)} custom-call(bf16[8,64,2048]{2,1,0:T(8,128)(2,1)} %bitcast.318), custom_call_target="tpu_custom_call" | custom-call | bytes 62914560 | tf_op jit(solution)/shard_map/pallas_call | solution.py:204
  343.5 24.7 %shard_map.137 = bf16[8,64,2048]{2,1,0:T(8,128)(2,1)} custom-call(bf16[64,2048]{1,0:T(8,128)(2,1)} %broadcast_21_carried_ref.2.carried_ref, bf16[64,2048]{1,0:T(8,128)(2,1)} %get-tuple-element.277.root_ref), custom_call_target="tpu_custom_call" | custom-call | bytes 62914560 | tf_op jit(solution)/shard_map/pallas_call | solution.py:135
  377.1 7.7 %convolution_convert_fusion.11 = bf16[512,2048]{1,0:T(8,128)(2,1)} fusion(bf16[512,128]{1,0:T(8,128)(2,1)S(1)} %select_convert_fusion.4, bf16[512,768]{1,0:T(8,128)(2,1)} %get-tuple-element.262, bf16[512,768]{1,0:T(8,128)(2,1)} %get-tuple-element.261, bf16[2048,8]{1,0:T(8,128)(2,1)} %bitcast.321, bf16[2048,768]{1,0:T(8,128)(2,1)} %bitcast.342, ...), kind=kOutput, calls=%fused_computation.187 | convolution fusion | flops 3523084288 | bytes 10125312 | tf_op jit(solution)/shard_map/dot_general | solution.py:22
  384.8 20.4 %shard_map.138 = bf16[4,64,2048]{2,1,0:T(8,128)(2,1)} custom-call(bf16[8,64,2048]{2,1,0:T(8,128)(2,1)} %bitcast.319), custom_call_target="tpu_custom_call" | custom-call | bytes 62914560 | tf_op jit(solution)/shard_map/pallas_call | solution.py:204
  410.7 21.6 %shard_map.139 = bf16[8,64,2048]{2,1,0:T(8,128)(2,1)} custom-call(bf16[64,2048]{1,0:T(8,128)(2,1)} %fusion.206.carried_ref, bf16[64,2048]{1,0:T(8,128)(2,1)} %get-tuple-element.276.root_ref), custom_call_target="tpu_custom_call" | custom-call | bytes 62914560 | tf_op jit(solution)/shard_map/pallas_call | solution.py:135
  449.7 21.5 %shard_map.140 = bf16[4,64,2048]{2,1,0:T(8,128)(2,1)} custom-call(bf16[8,64,2048]{2,1,0:T(8,128)(2,1)} %bitcast.312), custom_call_target="tpu_custom_call" | custom-call | bytes 62914560 | tf_op jit(solution)/shard_map/pallas_call | solution.py:204
  476.8 21.2 %shard_map.141 = bf16[8,64,2048]{2,1,0:T(8,128)(2,1)} custom-call(bf16[64,2048]{1,0:T(8,128)(2,1)} %fusion.208.carried_ref, bf16[64,2048]{1,0:T(8,128)(2,1)} %get-tuple-element.276.root_ref), custom_call_target="tpu_custom_call" | custom-call | bytes 62914560 | tf_op jit(solution)/shard_map/pallas_call | solution.py:135
  511.5 20.0 %shard_map.142 = bf16[4,64,2048]{2,1,0:T(8,128)(2,1)} custom-call(bf16[8,64,2048]{2,1,0:T(8,128)(2,1)} %bitcast.313), custom_call_target="tpu_custom_call" | custom-call | bytes 62914560 | tf_op jit(solution)/shard_map/pallas_call | solution.py:204
  537.0 19.9 %shard_map.143 = bf16[8,64,2048]{2,1,0:T(8,128)(2,1)} custom-call(bf16[64,2048]{1,0:T(8,128)(2,1)} %fusion.210.carried_ref, bf16[64,2048]{1,0:T(8,128)(2,1)} %get-tuple-element.276.root_ref), custom_call_target="tpu_custom_call" | custom-call | bytes 62914560 | tf_op jit(solution)/shard_map/pallas_call | solution.py:135
  572.2 20.0 %shard_map.144 = bf16[4,64,2048]{2,1,0:T(8,128)(2,1)} custom-call(bf16[8,64,2048]{2,1,0:T(8,128)(2,1)} %bitcast.311), custom_call_target="tpu_custom_call" | custom-call | bytes 62914560 | tf_op jit(solution)/shard_map/pallas_call | solution.py:204
  597.8 20.1 %shard_map.145 = bf16[8,64,2048]{2,1,0:T(8,128)(2,1)} custom-call(bf16[64,2048]{1,0:T(8,128)(2,1)} %fusion.212.carried_ref, bf16[64,2048]{1,0:T(8,128)(2,1)} %get-tuple-element.276.root_ref), custom_call_target="tpu_custom_call" | custom-call | bytes 62914560 | tf_op jit(solution)/shard_map/pallas_call | solution.py:135
  628.4 32.6 %conditional.1 = (f32[8,2048]{1,0:T(8,128)S(1)}, bf16[1,1,2048,768]{3,2,1,0:T(8,128)(2,1)}, bf16[1,1,2048,768]{3,2,1,0:T(8,128)(2,1)}, bf16[1,1,768,2048]{3,2,1,0:T(8,128)(2,1)}) conditional(s32[]{:T(128)} %clamp.3, (bf16[512,128]{1,0:T(8,128)(2,1)S(1)}, bf16[512,128]{1,0:T(8,128)(2,1)}, bf16[512,2048]{1,0:T(8,128)(2,1)}, ...), branch_computations={%region_42.43_spmd, %region_43.44_spmd, %region_44.45_spmd, %regio... | conditional | flops 9718779904 | bytes 92735784 | solution.py:347
  661.8 9.8 %shard_map.146 = f32[4,8,2048]{2,1,0:T(8,128)} custom-call(f32[8,8,2048]{2,1,0:T(8,128)} %broadcast_in_dim.165.parts_ref), custom_call_target="tpu_custom_call" | custom-call | bytes 7864320 | tf_op jit(solution)/shard_map/pallas_call | solution.py:204
  (334 shorter events, 229.8 us)
Async XLA Ops:
  7.2 51.8 %copy-start = (bf16[1,1,768,2048]{3,2,1,0:T(8,128)(2,1)S(1)}, bf16[1,1,768,2048]{3,2,1,0:T(8,128)(2,1)}, u32[]{:S(2)}) copy-start(bf16[1,1,768,2048]{3,2,1,0:T(8,128)(2,1)} %param.19) | copy-start | bytes 9437188
  7.2 666.1 %all-reduce.4.cloned.1.call-start = ((), (), s32[]{:S(2)}) async-start(), calls=%async_computation | async-start | bytes 2105344 | tf_op jit(solution)/shard_map/psum | solution.py:294
  34.8 15.5 %copy-start.33 = (bf16[1,2048,8]{1,2,0:T(8,128)(2,1)S(1)}, bf16[1,2048,8]{1,2,0:T(8,128)(2,1)}, u32[]{:S(2)}) copy-start(bf16[1,2048,8]{1,2,0:T(8,128)(2,1)} %param.15) | copy-start | bytes 98308
  51.6 6.9 %copy-start.80 = (f32[8,512]{1,0:T(8,128)}, f32[8,512]{1,0:T(8,128)S(1)}, u32[]{:S(2)}) copy-start(f32[8,512]{1,0:T(8,128)S(1)} %broadcast_divide_fusion.4) | copy-start | bytes 49156
  51.6 6.9 %copy-start.85 = (f32[1,512]{1,0:T(1,128)}, f32[1,512]{1,0:T(1,128)S(1)}, u32[]{:S(2)}) copy-start(f32[1,512]{1,0:T(1,128)S(1)} %constant_dynamic-slice_fusion.24) | copy-start | bytes 6148
  237.5 6.8 copy-start.83
  298.7 6.8 copy-start.84
  309.2 22.3 %copy-start.114 = (s32[2,64]{1,0:T(2,128)S(1)}, s32[2,64]{1,0:T(2,128)}, u32[]{:S(2)}) copy-start(s32[2,64]{1,0:T(2,128)} %param.14) | copy-start | bytes 1540
  309.2 24.9 %copy-start.50 = (bf16[64,2048]{1,0:T(8,128)(2,1)S(1)}, bf16[64,2048]{1,0:T(8,128)(2,1)}, u32[]{:S(2)}) copy-start(bf16[64,2048]{1,0:T(8,128)(2,1)} %get-tuple-element.268.carried_ref) | copy-start | bytes 786436
  341.2 28.3 %copy-start.94 = (f32[1,512]{1,0:T(1,128)S(1)}, f32[1,512]{1,0:T(1,128)}, u32[]{:S(2)}) copy-start(f32[1,512]{1,0:T(1,128)} %copy-done.93) | copy-start | bytes 6148
  377.1 7.7 %copy-start.66 = (bf16[512,128]{1,0:T(8,128)(2,1)}, bf16[512,128]{1,0:T(8,128)(2,1)S(1)}, u32[]{:S(2)}) copy-start(bf16[512,128]{1,0:T(8,128)(2,1)S(1)} %select_convert_fusion.4) | copy-start | bytes 393220
  384.8 21.8 %copy-start.101 = (f32[64]{0:T(128)S(1)}, f32[64]{0:T(128)}, u32[]{:S(2)}) copy-start(f32[64]{0:T(128)} %get-tuple-element.269) | copy-start | bytes 772
  405.2 27.1 %copy-start.92 = (f32[1,512]{1,0:T(1,128)S(1)}, f32[1,512]{1,0:T(1,128)}, u32[]{:S(2)}) copy-start(f32[1,512]{1,0:T(1,128)} %copy-done.91) | copy-start | bytes 6148
  407.4 30.4 %copy-start.95 = (bf16[8,64]{1,0:T(8,128)(2,1)}, bf16[8,64]{1,0:T(8,128)(2,1)S(1)}, u32[]{:S(2)}) copy-start(bf16[8,64]{1,0:T(8,128)(2,1)S(1)} %fusion.238) | copy-start | bytes 3076
  432.4 8.8 %copy-start.64 = (bf16[512,768]{1,0:T(8,128)(2,1)S(1)}, bf16[512,768]{1,0:T(8,128)(2,1)}, u32[]{:S(2)}) copy-start(bf16[512,768]{1,0:T(8,128)(2,1)} %get-tuple-element.261) | copy-start | bytes 2359300
  432.4 8.8 %copy-start.65 = (bf16[512,768]{1,0:T(8,128)(2,1)S(1)}, bf16[512,768]{1,0:T(8,128)(2,1)}, u32[]{:S(2)}) copy-start(bf16[512,768]{1,0:T(8,128)(2,1)} %get-tuple-element.262) | copy-start | bytes 2359300
  449.7 23.0 %copy-start.100 = (f32[64]{0:T(128)S(1)}, f32[64]{0:T(128)}, u32[]{:S(2)}) copy-start(f32[64]{0:T(128)} %get-tuple-element.267) | copy-start | bytes 772
  471.3 26.8 %copy-start.90 = (f32[1,512]{1,0:T(1,128)S(1)}, f32[1,512]{1,0:T(1,128)}, u32[]{:S(2)}) copy-start(f32[1,512]{1,0:T(1,128)} %copy-done.89) | copy-start | bytes 6148
  498.0 8.1 %copy-start.112 = (bf16[1,1,2048,768]{3,2,1,0:T(8,128)(2,1)S(1)}, bf16[1,1,2048,768]{3,2,1,0:T(8,128)(2,1)}, u32[]{:S(2)}) copy-start(bf16[1,1,2048,768]{3,2,1,0:T(8,128)(2,1)} %param.17) | copy-start | bytes 9437188
  511.5 21.5 %copy-start.99 = (f32[64]{0:T(128)S(1)}, f32[64]{0:T(128)}, u32[]{:S(2)}) copy-start(f32[64]{0:T(128)} %get-tuple-element.265) | copy-start | bytes 772
  531.5 25.5 %copy-start.88 = (f32[1,512]{1,0:T(1,128)S(1)}, f32[1,512]{1,0:T(1,128)}, u32[]{:S(2)}) copy-start(f32[1,512]{1,0:T(1,128)} %copy-done.87) | copy-start | bytes 6148
  557.0 9.9 %copy-start.113 = (bf16[1,1,2048,768]{3,2,1,0:T(8,128)(2,1)S(1)}, bf16[1,1,2048,768]{3,2,1,0:T(8,128)(2,1)}, u32[]{:S(2)}) copy-start(bf16[1,1,2048,768]{3,2,1,0:T(8,128)(2,1)} %param.17) | copy-start | bytes 9437188
  572.2 21.5 %copy-start.98 = (f32[64]{0:T(128)S(1)}, f32[64]{0:T(128)}, u32[]{:S(2)}) copy-start(f32[64]{0:T(128)} %get-tuple-element.263) | copy-start | bytes 772
  592.2 25.6 %copy-start.86 = (f32[1,512]{1,0:T(1,128)S(1)}, f32[1,512]{1,0:T(1,128)}, u32[]{:S(2)}) copy-start(f32[1,512]{1,0:T(1,128)} %copy-done.85) | copy-start | bytes 6148
  (65 other events, 235.0 us)
Sparse Core Ops, SparseCore 0:
  341.4 136.6 all-reduce.3
